TPU v7x, 256 devices: a whole 4x4x8 slice. The times are simulated.
256 devices in a mesh: cfg: 2 (over core), req: 8 (over z), seq: 16 (over y, x).
Axes of the slice: x: 4, y: 4, z: 8, core: 2. Of those that a mesh axis runs over, the one named last changes fastest.
Arguments:
- queries: bfloat16 [2, 8, 768, 1536], P('cfg', 'req', 'seq'), may hold values from -50 to 50
- text_cache: bfloat16 [2, 8, 2, 512, 1536], P('cfg', 'req'), may hold values from -6 to 6
- image_cache: bfloat16 [2, 8, 2, 768, 1536], P('cfg', 'req'), may hold values from -6 to 6
- fresh_kv: bfloat16 [2, 8, 2, 96, 1536], P('cfg', 'req', None, 'seq'), may hold values from -6 to 6
- fresh_slots: int32 [8, 96], P('req'), may hold values from 0 to 767, as said below
- fresh_pos: int32 [3, 8, 96], P(None, 'req', 'seq'), may hold values from 0 to 63
- image_len: int32 [8], replicated, may hold values from 384 to 768, as said below
- stream: bfloat16 [2, 8, 768, 3072], P('cfg', None, 'seq', 'req'), may hold values from -30 to 30
- modulation: float32 [2, 8, 4, 3072], replicated, may hold values from -4 to 4
- out_weight: bfloat16 [1536, 3072], P('seq', 'req'), may hold values from -0.15625 to 0.15625
- up_weight: bfloat16 [3072, 12288], P('seq', 'req'), may hold values from -0.109375 to 0.109375
- down_weight: bfloat16 [12288, 3072], P('req', 'seq'), may hold values from -0.0546875 to 0.0546875
- final_weight: bfloat16 [3072, 64], replicated, may hold values from -0.109375 to 0.109375
- latent: float32 [8, 384, 128], P('req', 'seq', 'cfg'), may hold values from -6 to 6
- step_index: int32 [1], replicated, may hold values from 0 to 27
Outputs:
- latent_next: float32 [8, 384, 128], P('req', 'seq', 'cfg')
- denoised: float32 [8, 384, 128], P('req', 'seq', 'cfg')
Inputs may be any that keep to these rules, and one draw needn't show every extreme that they name: `fresh_slots`: columns k * 6 to (k + 1) * 6 - 1 of a row hold distinct slots from k * 48 to (k + 1) * 48 - 1. `image_len`: some request has exactly 768 image tokens and some other exactly 384.
All inputs are finite; a program needn't handle non-finite values.
Results may differ from a plain program's by a relative error of at most 0.0095.
Values may be sent and summed in bfloat16 or wider, within the bound.
A program may use at most 128 MiB of HBM per device.

v0:
```python
import math

import jax
import jax.numpy as jnp
from jax import lax
from jax.sharding import PartitionSpec as P

STEPS = 28


GUIDANCE = 3.0
SHIFT = 3.0
SCALE = 1.0 / math.sqrt(128.0)
EPSILON = 1e-06


def swapped(block, axis, stride):
    count = lax.axis_size(axis)
    route = []
    for low in range(count):
        high = low | 1 << stride
        if high != low and high < count:
            route += [(low, high), (high, low)]
    return lax.ppermute(block, axis, route)


def rope_angles(positions):
    columns = []
    for component, axis_span in ((0, 16), (1, 56), (2, 56)):
        pair_ids = jnp.arange(axis_span // 2, dtype=jnp.float32)
        frequency = jnp.exp(-(2.0 * pair_ids / axis_span) * math.log(10000.0))
        columns.append(positions[component].astype(jnp.float32)[:, None] * frequency[None, :])
    return jnp.concatenate(columns, axis=1)


def rotate(key_rows, angles):
    row_total = key_rows.shape[0]
    paired = key_rows.reshape(row_total, -1, 64, 2)
    cosine = jnp.cos(angles)[:, None, :]
    sine = jnp.sin(angles)[:, None, :]
    first = cosine * paired[..., 0] - sine * paired[..., 1]
    second = sine * paired[..., 0] + cosine * paired[..., 1]
    return jnp.stack([first, second], axis=-1).reshape(row_total, -1)


def noise_level(index):
    fraction = 1.0 - index.astype(jnp.float32) / STEPS
    return SHIFT * fraction / (SHIFT * fraction + 1.0 - fraction)


def head_scores(query_heads, key_rows):
    key_heads = key_rows.reshape(key_rows.shape[0], -1, 128)
    return (
        jnp.einsum("qhd,khd->hqk", query_heads, key_heads, preferred_element_type=jnp.float32)
        * SCALE
    )


def head_mix(weights, value_rows):
    value_heads = value_rows.reshape(value_rows.shape[0], -1, 128)
    return jnp.einsum("hqk,khd->qhd", weights, value_heads, preferred_element_type=jnp.float32)


def per_device(
    queries,
    text_cache,
    image_cache,
    fresh_kv,
    fresh_slots,
    fresh_pos,
    image_len,
    stream,
    modulation,
    out_weight,
    up_weight,
    down_weight,
    final_weight,
    latent,
    step_index,
):
    cfg_id = lax.axis_index("cfg")
    req_id = lax.axis_index("req")
    seq_id = lax.axis_index("seq")
    query_rows = queries[0, 0]
    row_count = query_rows.shape[0]
    query_heads = query_rows.reshape(row_count, -1, 128)
    text_kv = text_cache[0, 0]
    image_kv = image_cache[0, 0]
    angles = rope_angles(fresh_pos[:, 0, :])
    fresh_keys = rotate(fresh_kv[0, 0, 0].astype(jnp.float32), angles).astype(jnp.bfloat16)
    fresh_pair = jnp.stack([fresh_keys, fresh_kv[0, 0, 1]], axis=0)
    all_fresh, proj_cols, up_cols, down_rows = (
        lax.all_gather(fresh_pair, "seq", axis=1, tiled=True),
        lax.all_gather(out_weight, "seq", axis=0, tiled=True),
        lax.all_gather(up_weight, "seq", axis=0, tiled=True),
        lax.all_gather(down_weight, "seq", axis=1, tiled=True),
    )
    image_kv = image_kv.at[:, fresh_slots[0], :].set(all_fresh)
    length = lax.dynamic_index_in_dim(image_len, req_id, 0, keepdims=False)
    image_total = image_kv.shape[1]
    text_scores = head_scores(query_heads, text_kv[0])
    text_best = jnp.max(text_scores, axis=-1, keepdims=True)
    live_keys = (jnp.arange(image_total) < length)[None, None, :]
    image_scores = jnp.where(live_keys, head_scores(query_heads, image_kv[0]), -jnp.inf)
    row_max = jnp.maximum(text_best, jnp.max(image_scores, axis=-1, keepdims=True))
    text_probs = jnp.exp(text_scores - row_max)
    image_probs = jnp.exp(image_scores - row_max)
    total = jnp.sum(text_probs, axis=-1) + jnp.sum(image_probs, axis=-1)
    mixed = head_mix(text_probs.astype(jnp.bfloat16), text_kv[1]) + head_mix(
        image_probs.astype(jnp.bfloat16), image_kv[1]
    )
    attended = (
        (mixed / jnp.transpose(total)[:, :, None]).reshape(row_count, -1).astype(jnp.bfloat16)
    )
    projected = jnp.dot(
        lax.all_gather(attended, "req", axis=0, tiled=True),
        proj_cols,
        preferred_element_type=jnp.float32,
    )
    requests = stream.shape[1]
    col_count = stream.shape[3]
    mod_half = lax.dynamic_index_in_dim(modulation, cfg_id, 0, keepdims=False)
    gate_cols = lax.dynamic_slice_in_dim(mod_half[:, 0, :], req_id * col_count, col_count, 1)
    residual = (
        stream[0].astype(jnp.float32)
        + gate_cols[:, None, :] * projected.reshape(requests, row_count, col_count)
    ).astype(jnp.bfloat16)
    full_rows = lax.all_gather(
        residual.reshape(requests * row_count, col_count), "req", axis=1, tiled=True
    )
    wide = full_rows.reshape(requests, row_count, -1).astype(jnp.float32)
    average = jnp.mean(wide, axis=-1, keepdims=True)
    centered = wide - average
    spread = jnp.mean(centered * centered, axis=-1, keepdims=True)
    normed = (
        centered * lax.rsqrt(spread + EPSILON) * (1.0 + mod_half[:, 2][:, None, :])
        + mod_half[:, 1][:, None, :]
    )
    normed = normed.astype(jnp.bfloat16).reshape(requests * row_count, -1)

    def rows_product(left_rows, right):
        return jnp.dot(left_rows, right, preferred_element_type=jnp.float32)

    pre_act = rows_product(normed, up_cols)
    activated = jax.nn.gelu(pre_act, approximate=True).astype(jnp.bfloat16)
    mlp_rows = lax.psum_scatter(
        rows_product(activated, down_rows).astype(jnp.bfloat16),
        "req",
        scatter_dimension=0,
        tiled=True,
    ).astype(jnp.float32)
    own_rows = lax.dynamic_slice_in_dim(full_rows, req_id * row_count, row_count, 0)
    gate_two = lax.dynamic_index_in_dim(mod_half[:, 3, :], req_id, 0, keepdims=False)
    block_out = (own_rows.astype(jnp.float32) + gate_two[None, :] * mlp_rows).astype(jnp.bfloat16)
    velocity = jnp.dot(block_out, final_weight, preferred_element_type=jnp.float32).reshape(
        row_count // 2, -1
    )
    lane_count = velocity.shape[1]
    half_lanes = lane_count // 2
    outgoing = lax.dynamic_slice_in_dim(velocity, (1 - cfg_id) * half_lanes, half_lanes, 1)
    own_part = lax.dynamic_slice_in_dim(velocity, cfg_id * half_lanes, half_lanes, 1)
    partner = swapped(outgoing, "cfg", 0)
    cond_part = jnp.where(cfg_id == 0, own_part, partner)
    uncond_part = jnp.where(cfg_id == 0, partner, own_part)
    guided = uncond_part + GUIDANCE * (cond_part - uncond_part)
    level_now = noise_level(step_index[0])
    level_next = noise_level(step_index[0] + 1)
    token_ids = (
        seq_id * row_count
        + 2 * jnp.arange(row_count // 2, dtype=jnp.int32)[:, None]
        + cfg_id
        + jnp.zeros((1, half_lanes), jnp.int32)
    )
    valid = token_ids < length
    current = latent[0]
    latent_next = jnp.where(valid, current + (level_next - level_now) * guided, current)
    denoised = jnp.where(valid, current - level_now * guided, current)
    return (latent_next[None], denoised[None])


def solution(mesh):
    in_specs = (
        P("cfg", "req", "seq", None),
        P("cfg", "req", None, None, None),
        P("cfg", "req", None, None, None),
        P("cfg", "req", None, "seq", None),
        P("req", None),
        P(None, "req", "seq"),
        P(),
        P("cfg", None, "seq", "req"),
        P(),
        P("seq", "req"),
        P("seq", "req"),
        P("req", "seq"),
        P(),
        P("req", "seq", "cfg"),
        P(),
    )
    out_specs = (P("req", "seq", "cfg"), P("req", "seq", "cfg"))
    return jax.shard_map(
        per_device, mesh=mesh, in_specs=in_specs, out_specs=out_specs, check_vma=False
    )
```

profile of v0, /device:TPU:1, one launch (start us, length us, event | category | flops | bytes accessed | tf_op | source)
XLA Modules:
  0.0 484.3 jit_solution(10954910353682535081)
XLA Ops:
  8.5 0.9 fusion.58
  9.7 1.0 multiply_subtract_fusion
  12.5 20.3 %all_gather.18 = bf16[2,96,1536]{2,0,1:T(2,128)(2,1)S(1)} all-gather(bf16[2,6,1536]{2,0,1:T(2,128)(2,1)S(1)} %pad_maximum_fusion.1), channel_id=1, replica_groups=mesh['cfg'=2,'req'=8,'seq'=16] {'seq'}, dimensions={1}, use_global_device_ids=true | all-gather | bytes 626688 | tf_op jit(solution)/shard_map/all_gather | solution.py:93
  32.8 9.4 %copy.107 = bf16[1,1,2,768,1536]{4,2,3,1,0:T(2,128)(2,1)} copy(bf16[1,1,2,768,1536]{4,3,2,1,0:T(8,128)(2,1)} %param.17) | data formatting | bytes 9437184 | tf_op args[2]
  42.2 11.7 %scatter_fusion = bf16[2,768,1536]{2,0,1:T(2,128)(2,1)} fusion(bf16[2,768,1536]{2,0,1:T(2,128)(2,1)} %bitcast.99, s32[96]{0:T(128)S(1)} %fusion.46, bf16[96,2,1536]{2,1,0:T(2,128)(2,1)S(1)} %bitcast.106), kind=kCustom, calls=%fused_computation | custom fusion | bytes 1769856 | tf_op jit(solution)/shard_map/scatter | solution.py:98
  53.9 10.7 %fusion.55 = (bf16[1,768,1536]{2,0,1:T(2,128)(2,1)}, bf16[1,768,1536]{2,0,1:T(2,128)(2,1)}) fusion(bf16[2,768,1536]{2,0,1:T(2,128)(2,1)} %scatter_fusion), kind=kLoop, calls=%fused_computation.100 | loop fusion | bytes 9437184 | tf_op jit(solution)/shard_map/slice | solution.py:110
  64.6 11.7 %copy.72 = bf16[1,768,1536]{1,2,0:T(8,128)(2,1)} copy(bf16[1,768,1536]{2,0,1:T(2,128)(2,1)} %get-tuple-element.3) | data formatting | bytes 4718592 | tf_op jit(solution)/shard_map/slice | solution.py:104
  77.6 0.8 reshape_squeeze.15
  78.4 3.7 fusion.56
  82.2 1.7 copy.87
  83.9 1.5 fusion.59
  86.3 1.3 copy-done.4
  87.5 1.2 fusion.15
  88.7 1.0 fusion.28
  89.7 1.7 copy.90
  91.4 1.4 convolution_bitcast_fusion.1
  92.9 11.8 %copy.77 = bf16[1,768,1536]{1,2,0:T(8,128)(2,1)} copy(bf16[1,768,1536]{2,0,1:T(2,128)(2,1)} %get-tuple-element.2) | data formatting | bytes 4718592 | tf_op jit(solution)/shard_map/slice | solution.py:110
  104.8 2.7 fusion.27
  109.2 0.9 fusion.57
  110.2 39.1 %all-gather.6.cloned.1.call-done = bf16[384,1536]{1,0:T(8,128)(2,1)} async-done(((bf16[48,1536]{1,0:T(8,128)(2,1)}), bf16[384,1536]{1,0:T(8,128)(2,1)}) %all-gather.6.cloned.1.call-update) | async-done | bytes 1179664 | tf_op jit(solution)/shard_map/all_gather | solution.py:116
  149.3 52.0 %all-gather.8.cloned.1.call-done = bf16[1536,384]{1,0:T(8,128)(2,1)} async-done(((bf16[96,384]{1,0:T(8,128)(2,1)}), bf16[1536,384]{1,0:T(8,128)(2,1)}) %all-gather.8.cloned.1.call-update) | async-done | bytes 1179664 | tf_op jit(solution)/shard_map/all_gather | solution.py:94
  201.4 3.1 fusion.18
  205.8 38.7 %all-gather.10.cloned.1.call-done = bf16[384,3072]{1,0:T(8,128)(2,1)} async-done(((bf16[384,384]{1,0:T(8,128)(2,1)}), bf16[384,3072]{1,0:T(8,128)(2,1)}) %all-gather.10.cloned.1.call-update) | async-done | bytes 2359312 | tf_op jit(solution)/shard_map/all_gather | solution.py:128
  244.5 2.2 convert_reduce_fusion
  247.6 2.6 fusion.5
  250.2 78.9 %all-gather.12.cloned.1.call-done = bf16[3072,1536]{1,0:T(8,128)(2,1)} async-done(((bf16[192,1536]{1,0:T(8,128)(2,1)}), bf16[3072,1536]{1,0:T(8,128)(2,1)}) %all-gather.12.cloned.1.call-update) | async-done | bytes 9437200 | tf_op jit(solution)/shard_map/all_gather | solution.py:95
  329.2 82.8 %all-gather.14.cloned.1.call-done = bf16[1536,3072]{0,1:T(8,128)(2,1)} async-done(((bf16[1536,192]{0,1:T(8,128)(2,1)}), bf16[1536,3072]{0,1:T(8,128)(2,1)}) %all-gather.14.cloned.1.call-update) | async-done | bytes 9437200 | tf_op jit(solution)/shard_map/all_gather | solution.py:96
  411.9 16.2 %convolution_convert_fusion = bf16[384,3072]{1,0:T(8,128)(2,1)} fusion(bf16[1536,3072]{0,1:T(8,128)(2,1)} %all-gather.14.cloned.1.call-done, bf16[384,3072]{1,0:T(8,128)(2,1)} %fusion.5, bf16[3072,1536]{1,0:T(8,128)(2,1)} %all-gather.12.cloned.1.call-done), kind=kOutput, calls=%fused_computation.10 | convolution fusion | flops 7254245376 | bytes 23592960 | tf_op jit(solution)/shard_map/dot_general | solution.py:142
  428.9 37.9 %reduce-scatter.2.cloned.1.call-done = bf16[48,3072]{1,0:T(8,128)(2,1)} async-done(((bf16[384,3072]{1,0:T(8,128)(2,1)}), bf16[48,3072]{1,0:T(8,128)(2,1)}) %reduce-scatter.2.cloned.1.call-update) | async-done | bytes 294928 | tf_op jit(solution)/shard_map/reduce_scatter | solution.py:146
  466.8 1.8 fusion.37
  469.5 5.2 %collective-permute-start = (f32[24,64]{1,0:T(8,128)S(1)}, f32[24,64]{1,0:T(8,128)S(1)}, u32[]{:S(2)}, u32[]{:S(2)}) collective-permute-start(f32[24,64]{1,0:T(8,128)S(1)} %constant_dynamic-slice_fusion), channel_id=1, source_target_pairs={{0,128},{128,0},{1,129},{129,1},{2,130},{130,2},{3,131},{131,3},{4... | collective-permute-start | bytes 18440 | tf_op jit(solution)/shard_map/ppermute | solution.py:24
  476.0 1.4 fusion.44
  (81 shorter events, 11.6 us)
Async XLA Ops:
  7.2 102.0 %copy-start = (f32[2,8,4,3072]{3,2,1,0:T(4,128)S(1)}, f32[2,8,4,3072]{3,2,1,0:T(4,128)}, u32[]{:S(2)}) copy-start(f32[2,8,4,3072]{3,2,1,0:T(4,128)} %param.23) | copy-start | bytes 2359300
  7.2 142.1 %all-gather.6.cloned.1.call-start = ((), (), s32[]{:S(2)}) async-start(), calls=%async_computation.1 | async-start | bytes 1327104 | tf_op jit(solution)/shard_map/all_gather | solution.py:116
  32.8 9.4 %copy-start.14 = (s32[1,96]{1,0:T(1,128)S(1)}, s32[1,96]{1,0:T(1,128)}, u32[]{:S(2)}) copy-start(s32[1,96]{1,0:T(1,128)} %param.19) | copy-start | bytes 1156
  64.6 11.8 %copy-start.15 = (s32[8]{0:T(128)S(1)}, s32[8]{0:T(128)}, u32[]{:S(2)}) copy-start(s32[8]{0:T(128)} %param.21) | copy-start | bytes 100
  64.6 13.0 %copy-start.10 = (bf16[1,1,48,1536]{3,2,1,0:T(8,128)(2,1)S(1)}, bf16[1,1,48,1536]{3,2,1,0:T(8,128)(2,1)}, u32[]{:S(2)}) copy-start(bf16[1,1,48,1536]{3,2,1,0:T(8,128)(2,1)} %param.15) | copy-start | bytes 442372
  77.6 7.9 %copy-start.12 = (pred[768]{0:T(1024)(128)(4,1)}, pred[768]{0:T(1024)(128)(4,1)S(1)}, u32[]{:S(2)}) copy-start(pred[768]{0:T(1024)(128)(4,1)S(1)} %iota_compare_fusion) | copy-start | bytes 2308
  83.9 1.8 copy-start.3
  83.9 1.8 copy-start.6
  86.2 1.3 copy-start.4
  92.9 11.9 %copy-start.11 = (f32[12,48]{1,0:T(8,128)S(1)}, f32[12,48]{1,0:T(8,128)}, u32[]{:S(2)}) copy-start(f32[12,48]{1,0:T(8,128)} %fusion.28) | copy-start | bytes 6916
  92.9 11.9 %copy-start.5 = (f32[12,768,48]{1,2,0:T(8,128)S(1)}, f32[12,768,48]{1,2,0:T(8,128)}, u32[]{:S(2)}) copy-start(f32[12,768,48]{1,2,0:T(8,128)} %copy-done.4) | copy-start | bytes 5308420
  92.9 11.9 %copy-start.9 = (f32[48,12,128]{2,0,1:T(8,128)S(1)}, f32[48,12,128]{2,0,1:T(8,128)}, u32[]{:S(2)}) copy-start(f32[48,12,128]{2,0,1:T(8,128)} %convolution_bitcast_fusion.1) | copy-start | bytes 884740
  92.9 11.9 %copy-start.13 = (pred[768]{0:T(1024)(128)(4,1)S(1)}, pred[768]{0:T(1024)(128)(4,1)}, u32[]{:S(2)}) copy-start(pred[768]{0:T(1024)(128)(4,1)} %copy-done.12) | copy-start | bytes 2308
  107.4 93.9 %copy-start.8 = (bf16[1,8,48,384]{3,2,1,0:T(8,128)(2,1)S(1)}, bf16[1,8,48,384]{3,2,1,0:T(8,128)(2,1)}, u32[]{:S(2)}) copy-start(bf16[1,8,48,384]{3,2,1,0:T(8,128)(2,1)} %param.22) | copy-start | bytes 884740
  108.2 93.2 %all-gather.8.cloned.1.call-start = ((), (), s32[]{:S(2)}) async-start(), calls=%async_computation.2 | async-start | bytes 1253376 | tf_op jit(solution)/shard_map/all_gather | solution.py:94
  108.9 135.6 %all-gather.10.cloned.1.call-start = ((), (), s32[]{:S(2)}) async-start(), calls=%async_computation.3 | async-start | bytes 2654208 | tf_op jit(solution)/shard_map/all_gather | solution.py:128
  204.5 124.6 %all-gather.12.cloned.1.call-start = ((), (), s32[]{:S(2)}) async-start(), calls=%async_computation.4 | async-start | bytes 10027008 | tf_op jit(solution)/shard_map/all_gather | solution.py:95
  205.1 206.8 %all-gather.14.cloned.1.call-start = ((), (), s32[]{:S(2)}) async-start(), calls=%async_computation.5 | async-start | bytes 10027008 | tf_op jit(solution)/shard_map/all_gather | solution.py:96
  205.7 261.1 %reduce-scatter.2.cloned.1.call-start = ((), (), s32[]{:S(2)}) async-start(), calls=%async_computation.6 | async-start | bytes 2654208 | tf_op jit(solution)/shard_map/reduce_scatter | solution.py:146
  244.5 2.4 copy-start.2
  411.9 65.5 %copy-start.1 = (f32[2,8,4,3072]{3,2,1,0:T(4,128)S(1)}, f32[2,8,4,3072]{3,2,1,0:T(4,128)}, u32[]{:S(2)}) copy-start(f32[2,8,4,3072]{3,2,1,0:T(4,128)} %param.23) | copy-start | bytes 2359300
  428.1 38.7 %copy-start.7 = (bf16[3072,64]{0,1:T(8,128)(2,1)S(1)}, bf16[3072,64]{0,1:T(8,128)(2,1)}, u32[]{:S(2)}) copy-start(bf16[3072,64]{0,1:T(8,128)(2,1)} %param.27) | copy-start | bytes 1179652
  469.5 6.5 %collective-permute-start = (f32[24,64]{1,0:T(8,128)S(1)}, f32[24,64]{1,0:T(8,128)S(1)}, u32[]{:S(2)}, u32[]{:S(2)}) collective-permute-start(f32[24,64]{1,0:T(8,128)S(1)} %constant_dynamic-slice_fusion), channel_id=1, source_target_pairs={{0,128},{128,0},{1,129},{129,1},{2,130},{130,2},{3,131},{131,3},{4... | collective-permute-start | bytes 18440 | tf_op jit(solution)/shard_map/ppermute | solution.py:24
Sparse Core Ops, SparseCore 0:
  108.3 40.9 all-gather.5
  151.7 49.5 all-gather.7
  204.7 39.7 all-gather.9
  246.8 82.3 all-gather.11
  331.4 80.4 all-gather.13
  428.2 38.5 reduce-scatter.1
where the time goes:
time: 486 us; the launch traced here: 484 us
  waiting for transfers between devices  331 us (68%)
  local copies, waits for them, and re-layouts  71.1 us (15%)
  matrix products  27.3 us (6%)
  blocking collectives  20.3 us (4%)
  between operations  15.2 us (3%)
  other arithmetic  13.6 us (3%)
  starting transfers between devices  5.61 us (1%)
    all_gather x1, waiting for transfers between devices, per_device(): lax.all_gather(down_weight, 'seq', axis=1, tiled=True)  82.8 us
    all_gather x1, waiting for transfers between devices, per_device(): lax.all_gather(up_weight, 'seq', axis=0, tiled=True)  78.9 us
    all_gather x1, waiting for transfers between devices, per_device(): lax.all_gather(out_weight, 'seq', axis=0, tiled=True)  52 us
    all_gather x1, waiting for transfers between devices, per_device(): lax.all_gather(attended, 'req', axis=0, tiled=True)  39.1 us
    all_gather x1, waiting for transfers between devices, per_device(): lax.all_gather(residual.reshape(requests * row_count, col_count), 'req',...  38.7 us
    reduce_scatter x1, waiting for transfers between devices, per_device(): lax.psum_scatter(rows_product(activated, down_rows).astype(jnp.bfloat16),...  37.9 us
    slice x2, local copies, waits for them, and re-layouts, per_device(): image_kv[1]  22.5 us
    all_gather x1, blocking collectives, per_device(): lax.all_gather(fresh_pair, 'seq', axis=1, tiled=True)  20.3 us
  transfers between devices with their start and end apart: 7, of which 6 were waited for; matrix products, arithmetic and copies ran while one was open for 2% of the time, Pallas kernels for 0%

commit v1 on v0

v1 whole, which is shorter than its diff:
```python
import functools
import math

import jax
import jax.numpy as jnp
from jax import lax
from jax.experimental import pallas as pl
from jax.experimental.pallas import tpu as pltpu
from jax.sharding import PartitionSpec as P

STEPS = 28
GUIDANCE = 3.0
SHIFT = 3.0
SCALE = 1.0 / math.sqrt(128.0)
EPSILON = 1e-06
MESH = pl.DeviceIdType.MESH
F32 = jnp.float32
BF16 = jnp.bfloat16
NEG = -jnp.inf

ITEMS = ("fresh", "out", "up", "down")
OPS = ("1R", "1L", "1RR", "1LL", "2R", "2L", "2RR", "2LL", "Xa", "Xb", "Xc", "Ya", "Yb", "Yc")
N_PLANE = len(ITEMS) * len(OPS)
RING_OPS = ("R1", "R2", "R3", "R4", "L1", "L2", "L3", "L4")
N_RING = 2 * len(RING_OPS)
N_VEL = 8
N_COPY = N_PLANE + N_RING + N_VEL + 1


def nt_dot(a, b):
    return lax.dot_general(a, b, (((1,), (1,)), ((), ())), preferred_element_type=F32)


def kernel(
    len_ref,
    lev_ref,
    q_hbm,
    text_hbm,
    img_hbm,
    fresh_ref,
    cs_ref,
    srow_ref,
    scol_ref,
    stream_ref,
    mod_hbm,
    out_hbm,
    up_hbm,
    down_hbm,
    wf_ref,
    lat_ref,
    next_ref,
    den_ref,
    q_ref,
    text,
    img,
    mod,
    fbuf,
    obuf,
    ubuf,
    dbuf,
    abuf,
    rbuf,
    nbuf,
    actbuf,
    att_o,
    att_m,
    att_l,
    vel,
    velin,
    vsum,
    vother,
    load_sem,
    send_sem,
    recv_sem,
):
    c = lax.axis_index("cfg")
    z = lax.axis_index("req")
    s = lax.axis_index("seq")
    y = s // 4
    x = s % 4

    def ring8(i):
        return lax.rem(z + i + 8, 8)

    started = []

    loads = {}

    def load(name, src, dst):
        loads[name] = pltpu.make_async_copy(src, dst, load_sem.at[len(loads)])
        loads[name].start()

    load("q", q_hbm, q_ref)
    load("tk", text_hbm.at[0], text.at[0])
    load("ik", img_hbm.at[0], img.at[0])
    load("tv", text_hbm.at[1], text.at[1])
    load("iv", img_hbm.at[1], img.at[1])
    load("o", out_hbm, obuf.at[y, x])
    load("u", up_hbm, ubuf.at[y, x])
    load("d", down_hbm, dbuf.at[y, x])
    load("mod", mod_hbm.at[c], mod)

    bufs = {"fresh": fbuf, "out": obuf, "up": ubuf, "down": dbuf}
    shards = {"out": out_hbm, "up": up_hbm, "down": down_hbm}

    def plane(item, op, core):
        buf = bufs[item]
        u, v = (x, y) if core == 0 else (y, x)
        own = () if item == "fresh" else (core,)

        def mod4(i):
            return lax.rem(i + 4, 4)

        def at(uu, vv, extra=()):
            where = (vv, uu) if core == 0 else (uu, vv)
            return buf.at[where + own + extra]

        def device(uu, vv):
            return {"seq": vv * 4 + uu if core == 0 else uu * 4 + vv}

        if item == "fresh":
            halves = ((slice(None), pl.ds(0, 768)), (slice(None), pl.ds(768, 768)))
        elif item == "out":
            halves = ((pl.ds(0, 32),), (pl.ds(32, 16),))
        else:
            halves = ((pl.ds(0, 48),), (pl.ds(48, 48),))
        right1, left1 = device(mod4(u + 1), v), device(mod4(u - 1), v)
        right2, left2 = device(u, mod4(v + 1)), device(u, mod4(v - 1))
        partner = {"cfg": 1 - core}
        every = slice(None)
        if op in ("1R", "1L"):
            dst = at(u, v)
            src = dst if item == "fresh" else shards[item].at[core]
            dev = right1 if op == "1R" else left1
        elif op == "1RR":
            src = dst = at(mod4(u - 1), v, halves[0])
            dev = right1
        elif op == "1LL":
            src = dst = at(mod4(u + 1), v, halves[1])
            dev = left1
        elif op in ("2R", "2L"):
            src = dst = at(every, v)
            dev = right2 if op == "2R" else left2
        elif op == "2RR":
            src = dst = at(pl.ds(0, 2), mod4(v - 1))
            dev = right2
        elif op == "2LL":
            src = dst = at(pl.ds(2, 2), mod4(v + 1))
            dev = left2
        else:
            step = {"a": -1, "b": 1, "c": 2}[op[1]]
            src = dst = at(mod4(u + step), v) if op[0] == "X" else at(every, mod4(v + step))
            dev = partner
        index = ITEMS.index(item) * len(OPS) + OPS.index(op)
        return pltpu.make_async_remote_copy(
            src_ref=src,
            dst_ref=dst,
            send_sem=send_sem.at[index],
            recv_sem=recv_sem.at[index],
            device_id=dev,
            device_id_type=MESH,
        )

    def arrival(item, op, core):
        buf = bufs[item]
        u, v = (x, y) if core == 0 else (y, x)
        return plane(item, op, core)

    plane_log = []

    def both(act):
        for core in (0, 1):
            pl.when(c == core)(functools.partial(act, core))

    def go(item, *ops):
        for op in ops:
            plane_log.append((item, op))

        def act(core):
            for op in ops:
                plane(item, op, core).start()

        both(act)

    def serve(item, steps):
        for _, after in steps:
            for op in after:
                plane_log.append((item, op))

        def act(core):
            for op, after in steps:
                plane(item, op, core).wait_recv()
                for follow in after:
                    plane(item, follow, core).start()

        both(act)

    def take(item, ops):
        def act(core):
            for op in ops:
                plane(item, op, 1 - core).wait_recv()

        both(act)

    def ring(which, op):
        buf = (abuf, rbuf)[which]
        k = int(op[1])
        right = op[0] == "R"
        owner = ring8(1 - k if right else k - 1)
        if k < 4:
            src = buf.at[owner]
        elif which == 0:
            src = buf.at[owner, :, pl.ds(0 if right else 768, 768)]
        else:
            src = buf.at[owner, pl.ds(0 if right else 4, 4)]
        index = N_PLANE + which * len(RING_OPS) + RING_OPS.index(op)
        return pltpu.make_async_remote_copy(
            src_ref=src,
            dst_ref=src,
            send_sem=send_sem.at[index],
            recv_sem=recv_sem.at[index],
            device_id={"req": ring8(1 if right else -1)},
            device_id_type=MESH,
        )

    def ring_go(which, *ops):
        for op in ops:
            ring(which, op).start()
            started.append(ring(which, op))

    lane = lax.broadcasted_iota(jnp.int32, (8, 128), 1)
    even = lax.rem(lane, 2) == 0
    cosine = cs_ref[0]
    sine = cs_ref[1]
    for h in range(12):
        k = fresh_ref[0, :, h * 128 : (h + 1) * 128].astype(F32)
        swapped = jnp.where(even, pltpu.roll(k, 127, 1), pltpu.roll(k, 1, 1))
        turned = k * cosine + swapped * sine
        v = fresh_ref[1, :, h * 128 : (h + 1) * 128].astype(F32)
        fbuf[y, x, :, h * 128 : (h + 1) * 128] = jnp.concatenate([turned, v], axis=0).astype(BF16)

    barrier = pltpu.get_barrier_semaphore()
    greeted = [{"cfg": 1 - c}]
    for step in (1, 3):
        greeted.append({"seq": y * 4 + lax.rem(x + step, 4)})
        greeted.append({"seq": lax.rem(y + step, 4) * 4 + x})
    for step in range(1, 8):
        greeted.append({"req": ring8(step)})
    for device in greeted:
        pl.semaphore_signal(barrier, inc=1, device_id=device, device_id_type=MESH)
    pl.semaphore_wait(barrier, len(greeted))

    go("fresh", "1R", "1L")

    length = len_ref[z]
    slot_hit = jnp.max(
        (scol_ref[...] == lax.broadcasted_iota(jnp.int32, (128, 768), 1)).astype(F32),
        axis=0,
        keepdims=True,
    )
    key_place = lax.broadcasted_iota(jnp.int32, (1, 768), 1)
    bias_img = jnp.where((key_place < length) & (slot_hit < 0.5), 0.0, NEG).astype(F32)
    slot_row = srow_ref[...]
    bias_new = jnp.where((slot_row >= 0) & (slot_row < length), 0.0, NEG).astype(F32)
    bias_new = jnp.broadcast_to(bias_new[0:1], (1, 128))

    def cached_heads(first, count):
        def one(h, carry):
            cols = pl.ds(pl.multiple_of(h * 128, 128), 128)
            q = q_ref[:, cols]
            st = nt_dot(q, text[0, :, cols]) * SCALE
            si = nt_dot(q, img[0, :, cols]) * SCALE + bias_img
            m = jnp.maximum(
                jnp.max(st, axis=-1, keepdims=True), jnp.max(si, axis=-1, keepdims=True)
            )
            pt = jnp.exp(st - m)
            pi = jnp.exp(si - m)
            total = jnp.sum(pt, axis=-1, keepdims=True) + jnp.sum(pi, axis=-1, keepdims=True)
            o = jnp.dot(pt.astype(BF16), text[1, :, cols], preferred_element_type=F32)
            o = o + jnp.dot(pi.astype(BF16), img[1, :, cols], preferred_element_type=F32)
            att_o[h] = o
            att_m[h] = jnp.broadcast_to(m, (48, 128))
            att_l[h] = jnp.broadcast_to(total, (48, 128))
            return carry

        lax.fori_loop(first, first + count, one, 0)

    for name in ("q", "tk", "ik", "tv", "iv"):
        loads[name].wait()
    cached_heads(0, 3)
    serve("fresh", [("1R", ["1RR"]), ("1L", ["1LL"])])
    go("out", "1R", "1L")
    go("up", "1R", "1L")
    cached_heads(3, 3)
    serve("fresh", [("1RR", []), ("1LL", ["2R", "2L"])])
    cached_heads(6, 3)
    serve("out", [("1R", ["1RR", "Xa"]), ("1L", ["1LL", "Xb"])])
    serve("fresh", [("2R", ["2RR"]), ("2L", ["2LL"])])
    go("down", "1R", "1L")
    cached_heads(9, 3)
    loads["o"].wait()
    serve("out", [("1RR", []), ("1LL", ["2R", "2L", "Xc"])])
    serve("fresh", [("2RR", []), ("2LL", [])])

    def fresh_head(h, carry):
        cols = pl.ds(pl.multiple_of(h * 128, 128), 128)
        q = q_ref[:, cols]
        kv = fbuf[:, :, :, cols].astype(F32)
        kf = kv[:, :, :8].reshape(128, 128).astype(BF16)
        vf = kv[:, :, 8:].reshape(128, 128).astype(BF16)
        sf = nt_dot(q, kf) * SCALE + bias_new
        before = att_m[h][:, 0:1]
        m = jnp.maximum(before, jnp.max(sf, axis=-1, keepdims=True))
        pf = jnp.exp(sf - m)
        keep = jnp.exp(before - m)
        total = att_l[h][:, 0:1] * keep + jnp.sum(pf, axis=-1, keepdims=True)
        o = att_o[h] * keep + jnp.dot(pf.astype(BF16), vf, preferred_element_type=F32)
        abuf[z, :, cols] = (o / total).astype(BF16)
        return carry

    lax.fori_loop(0, 12, fresh_head, 0)

    def project(r):
        rows = jnp.dot(abuf[r], obuf[...].reshape(1536, 384), preferred_element_type=F32)
        gate = mod[r, 0:1, pl.ds(pl.multiple_of(z * 384, 128), 384)]
        rbuf[z, r] = (stream_ref[r].astype(F32) + gate * rows).astype(BF16)

    ring_go(0, "R1", "L1")
    serve("out", [("2R", ["2RR", "Ya"]), ("2L", ["2LL", "Yb"])])
    serve("up", [("1R", ["1RR", "Xa"]), ("1L", ["1LL", "Xb"])])
    ring(0, "R1").wait_recv()
    ring_go(0, "R2")
    ring(0, "L1").wait_recv()
    ring_go(0, "L2")
    serve("out", [("2RR", []), ("2LL", ["Yc"])])
    loads["u"].wait()
    serve("up", [("1RR", []), ("1LL", ["2R", "2L", "Xc"])])
    take("out", ("Xa", "Xb", "Xc", "Ya", "Yb", "Yc"))
    loads["mod"].wait()
    project(z)
    ring(0, "R2").wait_recv()
    ring_go(0, "R3")
    ring(0, "L2").wait_recv()
    ring_go(0, "L3")
    serve("down", [("1R", ["1RR", "Xa"]), ("1L", ["1LL", "Xb"])])
    project(ring8(-1))
    project(ring8(1))
    ring(0, "R3").wait_recv()
    ring_go(0, "R4")
    ring(0, "L3").wait_recv()
    ring_go(0, "L4")
    loads["d"].wait()
    serve("down", [("1RR", []), ("1LL", ["2R", "2L", "Xc"])])
    project(ring8(-2))
    project(ring8(2))
    project(ring8(-3))
    project(ring8(3))
    ring(0, "R4").wait_recv()
    ring(0, "L4").wait_recv()
    project(ring8(4))

    ring_go(1, "R1", "L1")
    serve("up", [("2R", ["2RR", "Ya"]), ("2L", ["2LL", "Yb"])])
    ring(1, "R1").wait_recv()
    ring_go(1, "R2")
    ring(1, "L1").wait_recv()
    ring_go(1, "L2")
    ring(1, "R2").wait_recv()
    ring_go(1, "R3")
    ring(1, "L2").wait_recv()
    ring_go(1, "L3")
    serve("up", [("2RR", []), ("2LL", ["Yc"])])
    ring(1, "R3").wait_recv()
    ring_go(1, "R4")
    ring(1, "L3").wait_recv()
    ring_go(1, "L4")
    ring(1, "R4").wait_recv()
    ring(1, "L4").wait_recv()
    serve("down", [("2R", ["2RR", "Ya"]), ("2L", ["2LL", "Yb"])])

    def normalize(r, carry):
        parts = [rbuf[b, r].astype(F32) for b in range(8)]
        row_sum = sum(jnp.sum(p, axis=-1, keepdims=True) for p in parts)
        average = row_sum * (1.0 / 3072.0)
        centered = [p - average for p in parts]
        spread = sum(jnp.sum(p * p, axis=-1, keepdims=True) for p in centered) * (1.0 / 3072.0)
        inverse = lax.rsqrt(spread + EPSILON)
        for b in range(8):
            cols = pl.ds(b * 384, 384)
            gain = 1.0 + mod[r, 2:3, cols]
            shift = mod[r, 1:2, cols]
            nbuf[r, :, cols] = (centered[b] * inverse * gain + shift).astype(BF16)
        return carry

    lax.fori_loop(0, 8, normalize, 0)

    take("up", ("Xa", "Xb", "Xc", "Ya", "Yb", "Yc"))

    def up_tile(t, carry):
        cols = pl.ds(pl.multiple_of(t * 256, 256), 256)
        pre = jnp.dot(
            nbuf[...].reshape(384, 3072),
            ubuf[:, :, :, :, cols].reshape(3072, 256),
            preferred_element_type=F32,
        )
        actbuf[:, cols] = jax.nn.gelu(pre, approximate=True).astype(BF16)
        return carry

    lax.fori_loop(0, 6, up_tile, 0)
    serve("down", [("2RR", []), ("2LL", ["Yc"])])
    take("down", ("Xa", "Xb", "Xc", "Ya", "Yb", "Yc"))

    vel[...] = jnp.zeros_like(vel)

    def down_tile(t, carry):
        cols = pl.ds(pl.multiple_of(t * 768, 256), 768)
        mlp = nt_dot(actbuf[...], dbuf[t].reshape(768, 1536)).reshape(8, 48, 768)
        gated = (mlp * mod[:, 3:4, cols]).astype(BF16).reshape(384, 768)
        vel[:, :, 0:64] += nt_dot(gated, wf_ref[:, cols]).reshape(8, 48, 64)
        return carry

    lax.fori_loop(0, 4, down_tile, 0)

    def velocity_copy(step):
        target = ring8(step)
        index = N_PLANE + N_RING + step
        return pltpu.make_async_remote_copy(
            src_ref=vel.at[target],
            dst_ref=velin.at[step],
            send_sem=send_sem.at[index],
            recv_sem=recv_sem.at[index],
            device_id={"req": target},
            device_id_type=MESH,
        )

    for step in range(1, 8):
        velocity_copy(step).start()
        started.append(velocity_copy(step))
    own = jnp.concatenate([rbuf[b, z] for b in range(8)], axis=-1)
    total = vel[z][:, 0:64] + nt_dot(own, wf_ref[...])
    for step in range(1, 8):
        velocity_copy(step).wait_recv()
        total = total + velin[step][:, 0:64]
    vsum[:, 0:64] = total
    vsum[:, 64:128] = total
    swap = pltpu.make_async_remote_copy(
        src_ref=vsum,
        dst_ref=vother,
        send_sem=send_sem.at[N_COPY - 1],
        recv_sem=recv_sem.at[N_COPY - 1],
        device_id={"cfg": 1 - c},
        device_id_type=MESH,
    )
    swap.start()
    started.append(swap)
    swap.wait_recv()

    first = c == 0
    mine = jnp.where(first, vsum[pl.ds(0, 24, stride=2), :], vsum[pl.ds(1, 24, stride=2), :])
    theirs = jnp.where(first, vother[pl.ds(0, 24, stride=2), :], vother[pl.ds(1, 24, stride=2), :])
    cond = jnp.where(first, mine, theirs)[:, 0:64]
    uncond = jnp.where(first, theirs, mine)[:, 0:64]
    guided = uncond + GUIDANCE * (cond - uncond)
    token = s * 48 + 2 * lax.broadcasted_iota(jnp.int32, (24, 64), 0) + c
    valid = token < length
    current = lat_ref[...]
    now = lev_ref[0]
    later = lev_ref[1]
    next_ref[...] = jnp.where(valid, current + (later - now) * guided, current)
    den_ref[...] = jnp.where(valid, current - now * guided, current)

    def finish(core):
        for item, op in plane_log:
            plane(item, op, core).wait_send()

    both(finish)
    for copy in started:
        copy.wait_send()


def rope_tables(positions):
    lane = jnp.arange(128, dtype=jnp.int32)
    pair = lane // 2
    offset = jnp.where(pair < 8, 0, jnp.where(pair < 36, 8, 36))
    span = jnp.where(pair < 8, 16.0, 56.0).astype(F32)
    frequency = jnp.exp(-(2.0 * (pair - offset).astype(F32) / span) * math.log(10000.0))
    place = positions.astype(F32)[:, :, None]
    chosen = jnp.where(pair < 8, place[0], jnp.where(pair < 36, place[1], place[2]))
    angle = chosen * frequency
    sine = jnp.sin(angle)
    return jnp.stack([jnp.cos(angle), jnp.where(lane % 2 == 0, -sine, sine)])


def noise_level(index):
    fraction = 1.0 - index.astype(F32) / STEPS
    return SHIFT * fraction / (SHIFT * fraction + 1.0 - fraction)


def per_device(
    queries,
    text_cache,
    image_cache,
    fresh_kv,
    fresh_slots,
    fresh_pos,
    image_len,
    stream,
    modulation,
    out_weight,
    up_weight,
    down_weight,
    final_weight,
    latent,
    step_index,
):
    fresh = jnp.pad(fresh_kv[0, 0], ((0, 0), (0, 2), (0, 0)))
    tables = rope_tables(jnp.pad(fresh_pos[:, 0, :], ((0, 0), (0, 2))))
    slots = jnp.pad(fresh_slots.reshape(16, 6), ((0, 0), (0, 2)), constant_values=-1)
    index = step_index[0] + jnp.arange(2, dtype=jnp.int32)
    levels = noise_level(index)
    vmem = pl.BlockSpec(memory_space=pltpu.VMEM)
    smem = pl.BlockSpec(memory_space=pltpu.SMEM)
    hbm = pl.BlockSpec(memory_space=pl.ANY)
    out = jax.ShapeDtypeStruct((24, 64), F32)
    latent_next, denoised = pl.pallas_call(
        kernel,
        out_shape=(out, out),
        in_specs=[smem, smem, hbm, hbm, hbm, vmem, vmem, vmem, vmem, vmem, hbm, hbm, hbm, hbm, vmem, vmem],
        out_specs=(vmem, vmem),
        scratch_shapes=[
            pltpu.VMEM((48, 1536), BF16),
            pltpu.VMEM((2, 512, 1536), BF16),
            pltpu.VMEM((2, 768, 1536), BF16),
            pltpu.VMEM((8, 4, 3072), F32),
            pltpu.VMEM((4, 4, 16, 1536), BF16),
            pltpu.VMEM((4, 4, 2, 48, 384), BF16),
            pltpu.VMEM((4, 4, 2, 96, 1536), BF16),
            pltpu.VMEM((4, 4, 2, 96, 1536), BF16),
            pltpu.VMEM((8, 48, 1536), BF16),
            pltpu.VMEM((8, 8, 48, 384), BF16),
            pltpu.VMEM((8, 48, 3072), BF16),
            pltpu.VMEM((384, 1536), BF16),
            pltpu.VMEM((12, 48, 128), F32),
            pltpu.VMEM((12, 48, 128), F32),
            pltpu.VMEM((12, 48, 128), F32),
            pltpu.VMEM((8, 48, 128), F32),
            pltpu.VMEM((8, 48, 128), F32),
            pltpu.VMEM((48, 128), F32),
            pltpu.VMEM((48, 128), F32),
            pltpu.SemaphoreType.DMA((9,)),
            pltpu.SemaphoreType.DMA((N_COPY,)),
            pltpu.SemaphoreType.DMA((N_COPY,)),
        ],
        compiler_params=pltpu.CompilerParams(
            collective_id=0, has_side_effects=True, vmem_limit_bytes=60 * 1024 * 1024
        ),
    )(
        image_len,
        levels,
        queries[0, 0],
        text_cache[0, 0],
        image_cache[0, 0],
        fresh,
        tables,
        slots.reshape(1, 128),
        slots.reshape(128, 1),
        stream[0],
        modulation,
        out_weight.reshape(2, 48, 384),
        up_weight.reshape(2, 96, 1536),
        down_weight.T.reshape(2, 96, 1536),
        final_weight.T,
        latent[0],
    )
    return (latent_next[None], denoised[None])


def solution(mesh):
    in_specs = (
        P("cfg", "req", "seq", None),
        P("cfg", "req", None, None, None),
        P("cfg", "req", None, None, None),
        P("cfg", "req", None, "seq", None),
        P("req", None),
        P(None, "req", "seq"),
        P(),
        P("cfg", None, "seq", "req"),
        P(),
        P("seq", "req"),
        P("seq", "req"),
        P("req", "seq"),
        P(),
        P("req", "seq", "cfg"),
        P(),
    )
    out_specs = (P("req", "seq", "cfg"), P("req", "seq", "cfg"))
    return jax.shard_map(
        per_device, mesh=mesh, in_specs=in_specs, out_specs=out_specs, check_vma=False
    )
```

time: 486 us -> 121 us (0.25)
  waiting for transfers between devices: 331 us -> 0 us
  Pallas kernels: 0 us -> 110 us
  local copies, waits for them, and re-layouts: 71.1 us -> 6.63 us
  matrix products: 27.3 us -> 0 us
  blocking collectives: 20.3 us -> 0 us
  between operations: 15.2 us -> 1.3 us
  other arithmetic: 13.6 us -> 2.6 us
  starting transfers between devices: 5.61 us -> 0 us
    all_gather x5 -> x0, waiting for transfers between devices: 291 us -> none  [the longest x1 82.8 us: per_device(): lax.all_gather(down_weight, 'seq', axis=1, tiled=True)]
    pallas_call x0 -> x1, Pallas kernels: none -> 110 us  [per_device(): pl.pallas_call(kernel, out_shape=(out, out), in_specs=[smem, smem, hbm, h...]
    slice x5 -> x1, local copies, waits for them, and re-layouts: 38.9 us -> 0.01 us  [rope_tables(): place[0]]
    reduce_scatter x1 -> x0, waiting for transfers between devices: 37.9 us -> none  [per_device(): lax.psum_scatter(rows_product(activated, down_rows).astype(jnp.bfloat16),...]
    dot_general x7 -> x0, matrix products: 27.3 us -> none  [the longest x1 16.2 us: rows_product(): return jnp.dot(left_rows, right, preferred_element_type=jnp.float32)]
    all_gather x1 -> x0, blocking collectives: 20.3 us -> none  [per_device(): lax.all_gather(fresh_pair, 'seq', axis=1, tiled=True)]
    scatter x1 -> x0, local copies, waits for them, and re-layouts: 11.7 us -> none  [per_device(): image_kv = image_kv.at[:, fresh_slots[0], :].set(all_fresh)]
    unnamed x38 -> x5, local copies, waits for them, and re-layouts: 14.6 us -> 4.58 us
  transfers between devices with their start and end apart: 7 -> 0, of which waited for: 6 -> 0; matrix products, arithmetic and copies ran while one was open for 2% -> 0% of each run, Pallas kernels for 0% -> 0%
where the time goes in v1:
time: 121 us
  Pallas kernels  110 us (91%)
  local copies, waits for them, and re-layouts  6.63 us (5%)
  other arithmetic  2.6 us (2%)
  between operations  1.3 us (1%)
    pallas_call x1, Pallas kernels, per_device(): pl.pallas_call(kernel, out_shape=(out, out), in_specs=[smem, smem, hbm, h...  110 us
    unnamed x5, local copies, waits for them, and re-layouts  4.58 us

profile of v1, /device:TPU:1, one launch (start us, length us, event | category | flops | bytes accessed | tf_op | source)
XLA Modules:
  0.0 120.6 jit_solution(898314094634365916)
XLA Ops:
  1.3 0.5 subtract_divide_fusion.lev_ref
  1.8 0.5 broadcast.368
  2.3 1.3 %reduce.3 = s32[96]{0:T(128)S(1)} reduce(s32[1,96]{1,0:T(1,128)} %param.19, s32[]{:T(128)} %broadcast.368), dimensions={0}, to_apply=%param.19.reduce_sub_computation.3 | reduce | bytes 772 | tf_op args[4]
  3.7 0.7 copy.25
  4.4 0.1 fusion
  4.5 0.6 pad_maximum_fusion.cs_ref
  5.1 0.1 reshape.363
  5.2 0.6 reshape.364.srow_ref
  5.8 0.8 copy.24
  6.6 0.6 pad.12.fresh_ref
  7.2 0.7 reshape.369.scol_ref
  7.9 110.1 %shard_map.158 = (f32[24,64]{1,0:T(8,128)}, f32[24,64]{1,0:T(8,128)}) custom-call(s32[8]{0:T(128)} %len_ref.1, f32[2]{0:T(128)} %subtract_divide_fusion.lev_ref, bf16[48,1536]{1,0:T(8,128)(2,1)} %bitcast.34, bf16[2,512,1536]{2,1,0:T(8,128)(2,1)} %bitcast.28, bf16[2,768,1536]{2,1,0:T(8,128)(2,1)} %bitcast.27, bf16[2,8,1536]{2,1,0:T(8,128)(2,1)} %pad.12.fresh_ref, ...), custom_call_target="tpu_custom_call" | custom-call | tf_op jit(solution)/shard_map/pallas_call | solution.py:525
  118.0 1.3 %copy.29 = f32[1,24,64]{2,1,0:T(8,128)} copy(f32[1,24,64]{2,1,0:T(8,128)} %bitcast.38) | data formatting | bytes 12288
  119.3 1.3 %copy.30 = f32[1,24,64]{2,1,0:T(8,128)} copy(f32[1,24,64]{2,1,0:T(8,128)} %bitcast.37) | data formatting | bytes 12288
  (6 shorter events, 0.0 us)

commit v2 on v1

v2 whole, which is shorter than its diff:
```python
import functools
import math

import jax
import jax.numpy as jnp
from jax import lax
from jax.experimental import pallas as pl
from jax.experimental.pallas import tpu as pltpu
from jax.sharding import PartitionSpec as P

STEPS = 28
GUIDANCE = 3.0
SHIFT = 3.0
SCALE = 1.0 / math.sqrt(128.0)
EPSILON = 1e-06
MESH = pl.DeviceIdType.MESH
F32 = jnp.float32
BF16 = jnp.bfloat16
NEG = -jnp.inf
SKIP = frozenset()

ITEMS = ("fresh", "out", "up0", "up1", "down0", "down1")
OPS = ("1R", "1L", "1RR", "1LL", "2R", "2L", "2RR", "2LL", "Xa", "Xb", "Xc", "Ya", "Yb", "Yc")
N_PLANE = len(ITEMS) * len(OPS)
RING_OPS = ("R1", "R2", "R3", "R4", "L1", "L2", "L3", "L4")
N_RING = 4 * len(RING_OPS)
N_VEL = 8
N_COPY = N_PLANE + N_RING + N_VEL + 1


def nt_dot(a, b):
    return lax.dot_general(a, b, (((1,), (1,)), ((), ())), preferred_element_type=F32)


def nn_dot(a, b):
    return jnp.dot(a, b, preferred_element_type=F32)


def noise_level(index):
    fraction = 1.0 - index.astype(F32) / STEPS
    return SHIFT * fraction / (SHIFT * fraction + 1.0 - fraction)


def kernel(
    len_ref,
    step_ref,
    slot_ref,
    pos_ref,
    q_hbm,
    text_hbm,
    img_hbm,
    fresh_ref,
    stream_hbm,
    mod_hbm,
    out_hbm,
    up_hbm,
    down_hbm,
    wf_hbm,
    lat_ref,
    res_ref,
    q_ref,
    text,
    img,
    stream,
    mod,
    wf,
    ftmp,
    fbuf,
    obuf,
    ubuf,
    dbuf,
    abuf,
    rbuf,
    nbuf,
    actbuf,
    mlp,
    att_o,
    att_m,
    att_l,
    vel,
    swap_out,
    swap_in,
    part,
    partin,
    load_sem,
    send_sem,
    recv_sem,
):
    c = lax.axis_index("cfg")
    z = lax.axis_index("req")
    s = lax.axis_index("seq")
    y = s // 4
    x = s % 4

    def ring8(i):
        return lax.rem(z + i + 8, 8)

    started = []

    loads = {}

    def load(name, src, dst):
        loads[name] = pltpu.make_async_copy(src, dst, load_sem.at[len(loads)])
        loads[name].start()

    load("q", q_hbm, q_ref)
    load("tk", text_hbm.at[0], text.at[0])
    load("ik", img_hbm.at[0], img.at[0])
    load("tv", text_hbm.at[1], text.at[1])
    load("iv", img_hbm.at[1], img.at[1])
    load("out", out_hbm, obuf.at[y, x])
    for half in (0, 1):
        load("up%d" % half, up_hbm.at[:, :, pl.ds(768 * half, 768)], ubuf.at[half, y, x])
    for half in (0, 1):
        load("down%d" % half, down_hbm.at[:, :, pl.ds(768 * half, 768)], dbuf.at[half, y, x])
    load("stream", stream_hbm, stream)
    load("mod", mod_hbm.at[c], mod)
    load("wf", wf_hbm, wf)

    def plane(item, op, core):
        half = int(item[-1]) if item[-1] in "01" else 0
        if item == "fresh":
            buf, shard = fbuf, None
        elif item == "out":
            buf, shard = obuf, out_hbm.at[core]
        elif item[:2] == "up":
            buf, shard = ubuf.at[half], up_hbm.at[core, :, pl.ds(768 * half, 768)]
        else:
            buf, shard = dbuf.at[half], down_hbm.at[core, :, pl.ds(768 * half, 768)]
        u, v = (x, y) if core == 0 else (y, x)
        own = () if item == "fresh" else (core,)

        def mod4(i):
            return lax.rem(i + 4, 4)

        def at(uu, vv, extra=()):
            where = (vv, uu) if core == 0 else (uu, vv)
            return buf.at[where + own + extra]

        def device(uu, vv):
            return {"seq": vv * 4 + uu if core == 0 else uu * 4 + vv}

        if item == "fresh":
            halves = ((slice(None), pl.ds(0, 768)), (slice(None), pl.ds(768, 768)))
        elif item == "out":
            halves = ((pl.ds(0, 32),), (pl.ds(32, 16),))
        else:
            halves = ((pl.ds(0, 48),), (pl.ds(48, 48),))
        right1, left1 = device(mod4(u + 1), v), device(mod4(u - 1), v)
        right2, left2 = device(u, mod4(v + 1)), device(u, mod4(v - 1))
        every = slice(None)
        if op in ("1R", "1L"):
            dst = at(u, v)
            src = dst if item == "fresh" else shard
            dev = right1 if op == "1R" else left1
        elif op == "1RR":
            src = dst = at(mod4(u - 1), v, halves[0])
            dev = right1
        elif op == "1LL":
            src = dst = at(mod4(u + 1), v, halves[1])
            dev = left1
        elif op in ("2R", "2L"):
            src = dst = at(every, v)
            dev = right2 if op == "2R" else left2
        elif op == "2RR":
            src = dst = at(pl.ds(0, 2), mod4(v - 1))
            dev = right2
        elif op == "2LL":
            src = dst = at(pl.ds(2, 2), mod4(v + 1))
            dev = left2
        else:
            step = {"a": -1, "b": 1, "c": 2}[op[1]]
            src = dst = at(mod4(u + step), v) if op[0] == "X" else at(every, mod4(v + step))
            dev = {"cfg": 1 - core}
        index = ITEMS.index(item) * len(OPS) + OPS.index(op)
        return pltpu.make_async_remote_copy(
            src_ref=src,
            dst_ref=dst,
            send_sem=send_sem.at[index],
            recv_sem=recv_sem.at[index],
            device_id=dev,
            device_id_type=MESH,
        )

    plane_log = []

    def both(act):
        for core in (0, 1):
            pl.when(c == core)(functools.partial(act, core))

    def serve(*steps):
        steps = [step for step in steps if step[0] not in SKIP]
        for item, _, after in steps:
            plane_log.extend((item, op) for op in after.split())

        def act(core):
            for item, op, after in steps:
                if op:
                    plane(item, op, core).wait_recv()
                for follow in after.split():
                    plane(item, follow, core).start()

        if steps:
            both(act)

    def first(item):
        serve((item, None, "1R 1L"))

    def second(item):
        hand = item != "fresh"
        serve((item, "1R", "1RR Xa" if hand else "1RR"), (item, "1L", "1LL Xb" if hand else "1LL"))

    def third(item):
        if item in loads:
            loads[item].wait()
        hand = item != "fresh"
        serve((item, "1RR", ""), (item, "1LL", "2R 2L Xc" if hand else "2R 2L"))

    def fourth(item):
        hand = item != "fresh"
        serve((item, "2R", "2RR Ya" if hand else "2RR"), (item, "2L", "2LL Yb" if hand else "2LL"))

    def fifth(item):
        hand = item != "fresh"
        serve((item, "2RR", ""), (item, "2LL", "Yc" if hand else ""))

    def take(item):
        if item in SKIP:
            return

        def act(core):
            for op in ("Xa", "Xb", "Xc", "Ya", "Yb", "Yc"):
                plane(item, op, 1 - core).wait_recv()

        both(act)

    def ring(which, chunk, op):
        k = int(op[1])
        right = op[0] == "R"
        owner = ring8(1 - k if right else k - 1)
        if which == 0:
            src = abuf.at[owner, :, pl.ds(768 * chunk, 768)]
        else:
            src = rbuf.at[owner, pl.ds(4 * chunk, 4)]
        index = N_PLANE + (which * 2 + chunk) * len(RING_OPS) + RING_OPS.index(op)
        return pltpu.make_async_remote_copy(
            src_ref=src,
            dst_ref=src,
            send_sem=send_sem.at[index],
            recv_sem=recv_sem.at[index],
            device_id={"req": ring8(1 if right else -1)},
            device_id_type=MESH,
        )

    def ring_go(which, chunk, *ops):
        for op in ops:
            if "ring%d" % which not in SKIP:
                ring(which, chunk, op).start()
                started.append(ring(which, chunk, op))

    def hop(which, chunk, k):
        if "ring%d" % which in SKIP:
            return
        for side in "RL":
            if k < 4 or chunk == "RL".index(side):
                ring(which, chunk, side + str(k)).wait_recv()
            if k < 3 or (k == 3 and chunk == "RL".index(side)):
                ring_go(which, chunk, side + str(k + 1))

    barrier = pltpu.get_barrier_semaphore()
    greeted = [{"cfg": 1 - c}]
    for step in (1, 3):
        greeted.append({"seq": y * 4 + lax.rem(x + step, 4)})
        greeted.append({"seq": lax.rem(y + step, 4) * 4 + x})
    for step in range(1, 8):
        greeted.append({"req": ring8(step)})
    for device in greeted:
        pl.semaphore_signal(barrier, inc=1, device_id=device, device_id_type=MESH)

    lane = lax.broadcasted_iota(jnp.int32, (8, 128), 1)
    row = lax.broadcasted_iota(jnp.int32, (8, 128), 0)
    pair = lane // 2
    offset = jnp.where(pair < 8, 0, jnp.where(pair < 36, 8, 36))
    span = jnp.where(pair < 8, 16.0, 56.0)
    frequency = jnp.exp(-(2.0 * (pair - offset).astype(F32) / span) * math.log(10000.0))
    place = jnp.zeros((8, 128), F32)
    for j in range(6):
        ids = [jnp.full((8, 128), pos_ref[axis, 0, j], jnp.int32).astype(F32) for axis in range(3)]
        here = jnp.where(pair < 8, ids[0], jnp.where(pair < 36, ids[1], ids[2]))
        place = jnp.where(row == j, here, place)
    angle = place * frequency
    even = lax.rem(lane, 2) == 0
    cosine = jnp.cos(angle)
    sine = jnp.sin(angle)
    sine = jnp.where(even, -sine, sine)
    ftmp[...] = jnp.zeros_like(ftmp)
    for j in range(6):
        two = fresh_ref[j].astype(F32)
        ftmp[j : j + 1, :] = two[0:1]
        ftmp[8 + j : 9 + j, :] = two[1:2]
    for h in range(12):
        k = ftmp[0:8, h * 128 : (h + 1) * 128]
        swapped = jnp.where(even, pltpu.roll(k, 127, 1), pltpu.roll(k, 1, 1))
        turned = k * cosine + swapped * sine
        v = ftmp[8:16, h * 128 : (h + 1) * 128]
        fbuf[y, x, :, h * 128 : (h + 1) * 128] = jnp.concatenate([turned, v], axis=0).astype(BF16)

    pl.semaphore_wait(barrier, len(greeted))

    first("fresh")
    first("out")

    length = len_ref[z]
    key_place = lax.broadcasted_iota(jnp.int32, (8, 768), 1)
    new_place = lax.broadcasted_iota(jnp.int32, (8, 128), 1)

    def mark(k, carry):
        replaced, slots = carry
        for j in range(6):
            slot = slot_ref[0, k * 6 + j]
            replaced = jnp.where(key_place == slot, 1, replaced)
            slots = jnp.where(new_place == k * 8 + j, slot, slots)
        return replaced, slots

    replaced, slots = lax.fori_loop(
        0, 16, mark, (jnp.zeros((8, 768), jnp.int32), jnp.full((8, 128), -1, jnp.int32))
    )
    bias_img = jnp.where((key_place < length) & (replaced == 0), 0.0, NEG).astype(F32)[0:1]
    bias_new = jnp.where((slots >= 0) & (slots < length), 0.0, NEG).astype(F32)[0:1]

    def cached_heads(*heads):
        if "attn" in SKIP:
            return
        for h in heads:
            cols = pl.ds(h * 128, 128)
            q = q_ref[:, cols]
            st = nt_dot(q, text[0, :, cols]) * SCALE
            si = nt_dot(q, img[0, :, cols]) * SCALE + bias_img
            m = jnp.maximum(jnp.max(st, axis=-1, keepdims=True), jnp.max(si, axis=-1, keepdims=True))
            pt = jnp.exp(st - m)
            pi = jnp.exp(si - m)
            total = jnp.sum(pt, axis=-1, keepdims=True) + jnp.sum(pi, axis=-1, keepdims=True)
            o = nn_dot(pt.astype(BF16), text[1, :, cols]) + nn_dot(pi.astype(BF16), img[1, :, cols])
            att_o[h] = o
            att_m[h] = jnp.broadcast_to(m, (48, 128))
            att_l[h] = jnp.broadcast_to(total, (48, 128))

    def fresh_heads(*heads):
        if "attn" in SKIP:
            return
        for h in heads:
            cols = pl.ds(h * 128, 128)
            q = q_ref[:, cols]
            kv = fbuf[:, :, :, cols].astype(F32)
            kf = kv[:, :, :8].reshape(128, 128).astype(BF16)
            vf = kv[:, :, 8:].reshape(128, 128).astype(BF16)
            sf = nt_dot(q, kf) * SCALE + bias_new
            before = att_m[h][:, 0:1]
            m = jnp.maximum(before, jnp.max(sf, axis=-1, keepdims=True))
            pf = jnp.exp(sf - m)
            keep = jnp.exp(before - m)
            total = att_l[h][:, 0:1] * keep + jnp.sum(pf, axis=-1, keepdims=True)
            o = att_o[h] * keep + nn_dot(pf.astype(BF16), vf)
            abuf[z, :, cols] = (o / total).astype(BF16)

    def project(*steps):
        if "proj" in SKIP:
            return
        for step in steps:
            r = ring8(step)
            rows = nn_dot(abuf[r], obuf[...].reshape(1536, 384))
            gate = mod[r, 0:1, pl.ds(pl.multiple_of(z * 384, 128), 384)]
            rbuf[z, (step + 1) % 8] = (stream[r].astype(F32) + gate * rows).astype(BF16)

    def normalize(r, carry):
        parts = [rbuf[b, lax.rem(r - b + 9, 8)].astype(F32) for b in range(8)]
        row_sum = sum(jnp.sum(p, axis=-1, keepdims=True) for p in parts)
        average = row_sum * (1.0 / 3072.0)
        centered = [p - average for p in parts]
        spread = sum(jnp.sum(p * p, axis=-1, keepdims=True) for p in centered) * (1.0 / 3072.0)
        inverse = lax.rsqrt(spread + EPSILON)
        for b in range(8):
            cols = pl.ds(b * 384, 384)
            gain = 1.0 + mod[r, 2:3, cols]
            shift = mod[r, 1:2, cols]
            nbuf[r, :, cols] = (centered[b] * inverse * gain + shift).astype(BF16)
        return carry

    def up_half(half):
        def tile(t, carry):
            cols = pl.ds(pl.multiple_of(t * 256, 256), 256)
            weights = ubuf[half, :, :, :, :, cols].reshape(3072, 256)
            pre = nn_dot(nbuf[...].reshape(384, 3072), weights)
            actbuf[half, :, cols] = jax.nn.gelu(pre, approximate=True).astype(BF16)
            return carry

        if "mm" not in SKIP:
            lax.fori_loop(0, 3, tile, 0)

    def down_half(half):
        def tile(t, carry):
            cols = pl.ds(pl.multiple_of(t * 768, 256), 768)
            rows = nt_dot(actbuf[half], dbuf[half, t].reshape(768, 768)).reshape(8, 48, 768)
            if half == 0:
                mlp[:, :, cols] = rows
            else:
                rows = rows + mlp[:, :, cols]
                gated = (rows * mod[:, 3:4, cols]).astype(BF16).reshape(384, 768)
                vel[:, :, 0:64] += nt_dot(gated, wf[:, cols]).reshape(8, 48, 64)
            return carry

        if "mm" not in SKIP:
            lax.fori_loop(0, 4, tile, 0)

    for name in ("q", "tk", "ik", "tv", "iv"):
        loads[name].wait()
    cached_heads(0, 1, 2)
    second("fresh")
    first("up0")
    cached_heads(3, 4, 5)
    third("fresh")
    second("out")
    first("up1")
    cached_heads(6, 7, 8)
    third("out")
    second("up0")
    first("down0")
    cached_heads(9, 10, 11)
    fourth("fresh")
    third("up0")
    second("up1")
    fifth("fresh")
    fresh_heads(0, 1, 2, 3, 4, 5)
    ring_go(0, 0, "R1", "L1")
    fresh_heads(6, 7, 8, 9, 10, 11)
    ring_go(0, 1, "R1", "L1")
    fourth("out")
    third("up1")
    second("down0")
    first("down1")
    hop(0, 0, 1)
    hop(0, 1, 1)
    fifth("out")
    loads["stream"].wait()
    loads["mod"].wait()
    take("out")
    project(0)
    third("down0")
    hop(0, 0, 2)
    hop(0, 1, 2)
    project(-1, 1)
    second("down1")
    fourth("up0")
    hop(0, 0, 3)
    hop(0, 1, 3)
    project(2)
    ring_go(1, 0, "R1", "L1")
    project(-2)
    third("down1")
    hop(0, 0, 4)
    hop(0, 1, 4)
    project(3, 4, -3)
    ring_go(1, 1, "R1", "L1")
    fifth("up0")
    fourth("up1")
    hop(1, 0, 1)
    hop(1, 1, 1)
    fifth("up1")
    hop(1, 0, 2)
    hop(1, 1, 2)
    fourth("down0")
    hop(1, 0, 3)
    hop(1, 1, 3)
    fifth("down0")
    loads["wf"].wait()
    vel[...] = jnp.zeros_like(vel)
    hop(1, 0, 4)
    hop(1, 1, 4)
    fourth("down1")
    if "norm" not in SKIP:
        lax.fori_loop(0, 8, normalize, 0)
    own = jnp.concatenate([rbuf[b, lax.rem(z - b + 9, 8)] for b in range(8)], axis=-1)
    vel[z, :, 0:64] = nt_dot(own, wf[...])
    take("up0")
    up_half(0)
    take("up1")
    up_half(1)
    fifth("down1")
    take("down0")
    down_half(0)
    take("down1")
    down_half(1)

    even_core = c == 0
    scale = jnp.where(even_core, GUIDANCE, 1.0 - GUIDANCE)
    for r in range(8):
        evens = vel[r, pl.ds(0, 24, stride=2), :] * scale
        odds = vel[r, pl.ds(1, 24, stride=2), :] * scale
        part[r] = jnp.where(even_core, evens, odds)
        swap_out[r] = jnp.where(even_core, odds, evens)
    swap = pltpu.make_async_remote_copy(
        src_ref=swap_out,
        dst_ref=swap_in,
        send_sem=send_sem.at[N_COPY - 1],
        recv_sem=recv_sem.at[N_COPY - 1],
        device_id={"cfg": 1 - c},
        device_id_type=MESH,
    )
    swap.start()
    started.append(swap)
    swap.wait_recv()
    part[...] = part[...] + swap_in[...]

    def velocity_copy(step):
        target = ring8(step)
        index = N_PLANE + N_RING + step
        return pltpu.make_async_remote_copy(
            src_ref=part.at[target],
            dst_ref=partin.at[step],
            send_sem=send_sem.at[index],
            recv_sem=recv_sem.at[index],
            device_id={"req": target},
            device_id_type=MESH,
        )

    for step in (4, 3, 5, 2, 6, 1, 7):
        velocity_copy(step).start()
        started.append(velocity_copy(step))
    index = jnp.full((24, 64), step_ref[0], jnp.int32)
    now = noise_level(index)
    later = noise_level(index + 1)
    token = s * 48 + 2 * lax.broadcasted_iota(jnp.int32, (24, 64), 0) + c
    valid = token < length
    current = lat_ref[...]
    guided = part[z]
    for step in range(1, 8):
        velocity_copy(step).wait_recv()
        guided = guided + partin[step]
    guided = guided[:, 0:64]
    res_ref[0] = jnp.where(valid, current + (later - now) * guided, current)
    res_ref[1] = jnp.where(valid, current - now * guided, current)

    def finish(core):
        for item, op in plane_log:
            plane(item, op, core).wait_send()

    both(finish)
    for copy in started:
        copy.wait_send()


def per_device(
    queries,
    text_cache,
    image_cache,
    fresh_kv,
    fresh_slots,
    fresh_pos,
    image_len,
    stream,
    modulation,
    out_weight,
    up_weight,
    down_weight,
    final_weight,
    latent,
    step_index,
):
    vmem = pl.BlockSpec(memory_space=pltpu.VMEM)
    smem = pl.BlockSpec(memory_space=pltpu.SMEM)
    hbm = pl.BlockSpec(memory_space=pl.ANY)
    both = pl.pallas_call(
        kernel,
        out_shape=jax.ShapeDtypeStruct((2, 24, 64), F32),
        in_specs=[smem] * 4 + [hbm] * 3 + [vmem] + [hbm] * 6 + [vmem],
        out_specs=vmem,
        scratch_shapes=[
            pltpu.VMEM((48, 1536), BF16),
            pltpu.VMEM((2, 512, 1536), BF16),
            pltpu.VMEM((2, 768, 1536), BF16),
            pltpu.VMEM((8, 48, 384), BF16),
            pltpu.VMEM((8, 4, 3072), F32),
            pltpu.VMEM((64, 3072), BF16),
            pltpu.VMEM((16, 1536), F32),
            pltpu.VMEM((4, 4, 16, 1536), BF16),
            pltpu.VMEM((4, 4, 2, 48, 384), BF16),
            pltpu.VMEM((2, 4, 4, 2, 96, 768), BF16),
            pltpu.VMEM((2, 4, 4, 2, 96, 768), BF16),
            pltpu.VMEM((8, 48, 1536), BF16),
            pltpu.VMEM((8, 8, 48, 384), BF16),
            pltpu.VMEM((8, 48, 3072), BF16),
            pltpu.VMEM((2, 384, 768), BF16),
            pltpu.VMEM((8, 48, 3072), F32),
            pltpu.VMEM((12, 48, 128), F32),
            pltpu.VMEM((12, 48, 128), F32),
            pltpu.VMEM((12, 48, 128), F32),
            pltpu.VMEM((8, 48, 128), F32),
            pltpu.VMEM((8, 24, 128), F32),
            pltpu.VMEM((8, 24, 128), F32),
            pltpu.VMEM((8, 24, 128), F32),
            pltpu.VMEM((8, 24, 128), F32),
            pltpu.SemaphoreType.DMA((13,)),
            pltpu.SemaphoreType.DMA((N_COPY,)),
            pltpu.SemaphoreType.DMA((N_COPY,)),
        ],
        compiler_params=pltpu.CompilerParams(
            collective_id=0, has_side_effects=True, vmem_limit_bytes=60 * 1024 * 1024
        ),
    )(
        image_len,
        step_index,
        fresh_slots,
        fresh_pos,
        queries[0, 0],
        text_cache[0, 0],
        image_cache[0, 0],
        fresh_kv[0, 0].transpose(1, 0, 2),
        stream[0],
        modulation,
        out_weight.reshape(2, 48, 384),
        up_weight.reshape(2, 96, 1536),
        down_weight.T.reshape(2, 96, 1536),
        final_weight.T,
        latent[0],
    )
    return (both[0][None], both[1][None])


def solution(mesh):
    in_specs = (
        P("cfg", "req", "seq", None),
        P("cfg", "req", None, None, None),
        P("cfg", "req", None, None, None),
        P("cfg", "req", None, "seq", None),
        P("req", None),
        P(None, "req", "seq"),
        P(),
        P("cfg", None, "seq", "req"),
        P(),
        P("seq", "req"),
        P("seq", "req"),
        P("req", "seq"),
        P(),
        P("req", "seq", "cfg"),
        P(),
    )
    out_specs = (P("req", "seq", "cfg"), P("req", "seq", "cfg"))
    return jax.shard_map(
        per_device, mesh=mesh, in_specs=in_specs, out_specs=out_specs, check_vma=False
    )
```

time: 121 us -> 105 us (0.87)
  Pallas kernels: 110 us -> 102 us
  local copies, waits for them, and re-layouts: 6.63 us -> 1.33 us
  other arithmetic: 2.6 us -> 0 us
    pallas_call x1, Pallas kernels: 110 us -> 102 us  [per_device(): pl.pallas_call(kernel, out_shape=jax.ShapeDtypeStruct((2, 24, 64), F32),...]
    unnamed x5 -> x0, local copies, waits for them, and re-layouts: 4.58 us -> none
    reshape x3 -> x0, local copies, waits for them, and re-layouts: 1.41 us -> none  [the longest x1 0.69 us: per_device(): slots.reshape(128, 1)]
    slice x1, local copies, waits for them, and re-layouts: 0.01 us -> 1.33 us  [per_device(): return (both[0][None], both[1][None])]
    unnamed x1 -> x0, other arithmetic: 1.32 us -> none
where the time goes in v2:
time: 105 us
  Pallas kernels  102 us (97%)
  local copies, waits for them, and re-layouts  1.33 us (1%)
  between operations  1.29 us (1%)
    pallas_call x1, Pallas kernels, per_device(): pl.pallas_call(kernel, out_shape=jax.ShapeDtypeStruct((2, 24, 64), F32),...  102 us

profile of v2, /device:TPU:1, one launch (start us, length us, event | category | flops | bytes accessed | tf_op | source)
XLA Modules:
  0.0 104.8 jit_solution(7701813004167523553)
XLA Ops:
  1.3 102.2 %shard_map.158 = f32[2,24,64]{2,1,0:T(8,128)} custom-call(s32[8]{0:T(128)} %len_ref.1, s32[1]{0:T(128)S(6)} %copy.17.step_ref, s32[1,96]{1,0:T(1,128)} %slot_ref.1, s32[3,1,6]{2,1,0:T(1,128)} %pos_ref.1, bf16[48,1536]{1,0:T(8,128)(2,1)} %bitcast.20, bf16[2,512,1536]{2,1,0:T(8,128)(2,1)} %bitcast.15, bf16[2,768,1536]{2,1,0:T(8,128)(2,1)} %bitcast.14, ...), custom_call_target="tpu_custom_call" | custom-call | tf_op jit(solution)/shard_map/pallas_call | solution.py:572
  103.5 1.3 %fusion = (f32[1,24,64]{2,1,0:T(8,128)}, f32[1,24,64]{2,1,0:T(8,128)}) fusion(f32[2,24,64]{2,1,0:T(8,128)} %shard_map.158), kind=kLoop, calls=%fused_computation | loop fusion | bytes 24576 | tf_op jit(solution)/shard_map/slice | solution.py:626

commit v3 on v2

--- a/solution.py
+++ b/solution.py
@@ -19,13 +19,15 @@
 NEG = -jnp.inf
 SKIP = frozenset()
 
-ITEMS = ("fresh", "out", "up0", "up1", "down0", "down1")
+ITEMS = ("fresh", "out", "up0", "up1")
 OPS = ("1R", "1L", "1RR", "1LL", "2R", "2L", "2RR", "2LL", "Xa", "Xb", "Xc", "Ya", "Yb", "Yc")
 N_PLANE = len(ITEMS) * len(OPS)
 RING_OPS = ("R1", "R2", "R3", "R4", "L1", "L2", "L3", "L4")
 N_RING = 4 * len(RING_OPS)
 N_VEL = 8
-N_COPY = N_PLANE + N_RING + N_VEL + 1
+FOLD_OPS = ("1R", "1L", "2R", "2L", "3R", "3L", "4R", "4L", "5R", "5L", "5RR", "5LL", "6R", "6L", "6RR", "6LL")
+N_FOLD = len(FOLD_OPS)
+N_COPY = N_PLANE + N_RING + N_VEL + N_FOLD + 1
 
 
 def nt_dot(a, b):
@@ -68,12 +70,18 @@
     fbuf,
     obuf,
     ubuf,
-    dbuf,
+    down,
+    gpart,
+    gmid,
+    gfull,
+    gin1,
+    gin2,
+    gin3,
+    gin4,
     abuf,
     rbuf,
     nbuf,
     actbuf,
-    mlp,
     att_o,
     att_m,
     att_l,
@@ -111,8 +119,7 @@
     load("out", out_hbm, obuf.at[y, x])
     for half in (0, 1):
         load("up%d" % half, up_hbm.at[:, :, pl.ds(768 * half, 768)], ubuf.at[half, y, x])
-    for half in (0, 1):
-        load("down%d" % half, down_hbm.at[:, :, pl.ds(768 * half, 768)], dbuf.at[half, y, x])
+    load("down", down_hbm, down)
     load("stream", stream_hbm, stream)
     load("mod", mod_hbm.at[c], mod)
     load("wf", wf_hbm, wf)
@@ -123,10 +130,8 @@
             buf, shard = fbuf, None
         elif item == "out":
             buf, shard = obuf, out_hbm.at[core]
-        elif item[:2] == "up":
+        else:
             buf, shard = ubuf.at[half], up_hbm.at[core, :, pl.ds(768 * half, 768)]
-        else:
-            buf, shard = dbuf.at[half], down_hbm.at[core, :, pl.ds(768 * half, 768)]
         u, v = (x, y) if core == 0 else (y, x)
         own = () if item == "fresh" else (core,)
 
@@ -234,6 +239,111 @@
 
         both(act)
 
+    def fold(op, core):
+        u, v = (x, y) if core == 0 else (y, x)
+
+        def mod4(i):
+            return lax.rem(i + 4, 4)
+
+        right = "R" in op
+        one = 1 if right else -1
+        along_u = op[0] in "126"
+        uu, vv = (mod4(u + one), v) if along_u else (u, mod4(v + one))
+        dev = {"seq": vv * 4 + uu if core == 0 else uu * 4 + vv}
+        side = 0 if right else 1
+        if op[0] == "1":
+            src, dst = gpart.at[mod4(u + 2), pl.ds(2 * side, 2)], gin1.at[side]
+        elif op[0] == "2":
+            src, dst = gpart.at[mod4(u + one)], gin2.at[side]
+        elif op[0] == "3":
+            src, dst = gmid.at[mod4(v + 2), pl.ds(16 * side, 16)], gin3.at[side]
+        elif op[0] == "4":
+            src, dst = gmid.at[mod4(v + one)], gin4.at[side]
+        elif op[0] == "5":
+            src = gfull.at[u, v] if len(op) == 2 else gfull.at[u, mod4(v - one), pl.ds(16 * side, 16)]
+            dst = src
+        else:
+            src = gfull.at[u] if len(op) == 2 else gfull.at[mod4(u - one), pl.ds(2 * side, 2)]
+            dst = src
+        index = N_PLANE + N_RING + N_VEL + FOLD_OPS.index(op)
+        return pltpu.make_async_remote_copy(
+            src_ref=src,
+            dst_ref=dst,
+            send_sem=send_sem.at[index],
+            recv_sem=recv_sem.at[index],
+            device_id=dev,
+            device_id_type=MESH,
+        )
+
+    fold_log = []
+
+    def fold_step(*steps):
+        if "fold" in SKIP:
+            return
+        for _, _, after in steps:
+            fold_log.extend(after.split())
+
+        def act(core):
+            for op, add, after in steps:
+                if op:
+                    fold(op, core).wait_recv()
+                if add:
+                    add(core)
+                for follow in after.split():
+                    fold(follow, core).start()
+
+        both(act)
+
+    def across(core, step):
+        u, v = (x, y) if core == 0 else (y, x)
+        return lax.rem(u + step + 4, 4), lax.rem(v + step + 4, 4)
+
+    def add1(side):
+        def add(core):
+            u = across(core, 1 - 2 * side)[0]
+            for i in range(2):
+                place = 2 * side + i
+                total = gpart[u, place].astype(F32) + gin1[side, i].astype(F32)
+                gpart[u, place] = total.astype(BF16)
+
+        return add
+
+    def add2(core):
+        u = across(core, 0)[0]
+        for i in range(4):
+            total = gpart[u, i].astype(F32) + gin2[0, i].astype(F32) + gin2[1, i].astype(F32)
+            gmid[i] = total.astype(BF16)
+
+    def add3(side):
+        def add(core):
+            v = across(core, 1 - 2 * side)[1]
+            rows = pl.ds(16 * side, 16)
+            gmid[v, rows] = (gmid[v, rows].astype(F32) + gin3[side].astype(F32)).astype(BF16)
+
+        return add
+
+    def add4(core):
+        u, v = across(core, 0)
+        total = gmid[v].astype(F32) + gin4[0].astype(F32) + gin4[1].astype(F32)
+        gfull[u, v] = total.astype(BF16)
+
+    def fold_local():
+        if "fold" in SKIP:
+            return
+        window = pl.ds(pl.multiple_of((s // 2) * 384, 128), 384)
+        odd = s % 2 == 1
+
+        def mine(block):
+            return jnp.where(odd, pltpu.roll(block, 192, 1), block)[:, 0:192]
+
+        final = mine(wf[:, window].astype(F32))
+        down_rows = down[...].reshape(192, 1536)
+        for r in range(8):
+            gate = mine(jnp.broadcast_to(mod[r, 3:4, window], (8, 384)))[0:1]
+            product = nn_dot((final * gate).astype(BF16), down_rows)
+            gpart[r // 2, 2 * (r % 2)] = product[0:32].astype(BF16)
+            gpart[r // 2, 2 * (r % 2) + 1] = product[32:64].astype(BF16)
+
     def ring(which, chunk, op):
         k = int(op[1])
         right = op[0] == "R"
@@ -397,20 +507,12 @@
         if "mm" not in SKIP:
             lax.fori_loop(0, 3, tile, 0)
 
-    def down_half(half):
-        def tile(t, carry):
-            cols = pl.ds(pl.multiple_of(t * 768, 256), 768)
-            rows = nt_dot(actbuf[half], dbuf[half, t].reshape(768, 768)).reshape(8, 48, 768)
-            if half == 0:
-                mlp[:, :, cols] = rows
-            else:
-                rows = rows + mlp[:, :, cols]
-                gated = (rows * mod[:, 3:4, cols]).astype(BF16).reshape(384, 768)
-                vel[:, :, 0:64] += nt_dot(gated, wf[:, cols]).reshape(8, 48, 64)
-            return carry
-
-        if "mm" not in SKIP:
-            lax.fori_loop(0, 4, tile, 0)
+    def velocity(r, carry):
+        fold_r = gfull[lax.div(r, 2), pl.ds(2 * lax.rem(r, 2), 2)].reshape(64, 1536)
+        rows = nt_dot(actbuf[0, pl.ds(r * 48, 48)], fold_r[:, 0:768])
+        rows += nt_dot(actbuf[1, pl.ds(r * 48, 48)], fold_r[:, 768:1536])
+        vel[r, :, 0:64] += rows
+        return carry
 
     for name in ("q", "tk", "ik", "tv", "iv"):
         loads[name].wait()
@@ -424,7 +526,6 @@
     cached_heads(6, 7, 8)
     third("out")
     second("up0")
-    first("down0")
     cached_heads(9, 10, 11)
     fourth("fresh")
     third("up0")
@@ -436,27 +537,25 @@
     ring_go(0, 1, "R1", "L1")
     fourth("out")
     third("up1")
-    second("down0")
-    first("down1")
+    for name in ("stream", "mod", "wf", "down"):
+        loads[name].wait()
     hop(0, 0, 1)
     hop(0, 1, 1)
     fifth("out")
-    loads["stream"].wait()
-    loads["mod"].wait()
+    fold_local()
+    fold_step((None, None, "1R 1L"))
     take("out")
     project(0)
-    third("down0")
     hop(0, 0, 2)
     hop(0, 1, 2)
     project(-1, 1)
-    second("down1")
     fourth("up0")
     hop(0, 0, 3)
     hop(0, 1, 3)
     project(2)
     ring_go(1, 0, "R1", "L1")
     project(-2)
-    third("down1")
+    fold_step(("1R", add1(0), "2R"), ("1L", add1(1), "2L"))
     hop(0, 0, 4)
     hop(0, 1, 4)
     project(3, 4, -3)
@@ -465,31 +564,31 @@
     fourth("up1")
     hop(1, 0, 1)
     hop(1, 1, 1)
+    fold_step(("2R", None, ""), ("2L", add2, "3R 3L"))
+    hop(1, 0, 2)
+    fold_step(("3R", add3(0), "4R"), ("3L", add3(1), "4L"))
+    hop(1, 1, 2)
+    fold_step(("4R", None, ""), ("4L", add4, "5R 5L"))
     fifth("up1")
-    hop(1, 0, 2)
-    hop(1, 1, 2)
-    fourth("down0")
+    vel[...] = jnp.zeros_like(vel)
     hop(1, 0, 3)
+    fold_step(("5R", None, "5RR"), ("5L", None, "5LL"))
     hop(1, 1, 3)
-    fifth("down0")
-    loads["wf"].wait()
-    vel[...] = jnp.zeros_like(vel)
+    fold_step(("5RR", None, ""), ("5LL", None, "6R 6L"))
     hop(1, 0, 4)
     hop(1, 1, 4)
-    fourth("down1")
     if "norm" not in SKIP:
         lax.fori_loop(0, 8, normalize, 0)
+    fold_step(("6R", None, "6RR"), ("6L", None, "6LL"))
     own = jnp.concatenate([rbuf[b, lax.rem(z - b + 9, 8)] for b in range(8)], axis=-1)
     vel[z, :, 0:64] = nt_dot(own, wf[...])
     take("up0")
     up_half(0)
     take("up1")
     up_half(1)
-    fifth("down1")
-    take("down0")
-    down_half(0)
-    take("down1")
-    down_half(1)
+    fold_step(("6RR", None, ""), ("6LL", None, ""))
+    if "mm" not in SKIP:
+        lax.fori_loop(0, 8, velocity, 0)
 
     even_core = c == 0
     scale = jnp.where(even_core, GUIDANCE, 1.0 - GUIDANCE)
@@ -543,6 +642,8 @@
     def finish(core):
         for item, op in plane_log:
             plane(item, op, core).wait_send()
+        for op in fold_log:
+            fold(op, core).wait_send()
 
     both(finish)
     for copy in started:
@@ -585,12 +686,18 @@
             pltpu.VMEM((4, 4, 16, 1536), BF16),
             pltpu.VMEM((4, 4, 2, 48, 384), BF16),
             pltpu.VMEM((2, 4, 4, 2, 96, 768), BF16),
-            pltpu.VMEM((2, 4, 4, 2, 96, 768), BF16),
+            pltpu.VMEM((2, 96, 1536), BF16),
+            pltpu.VMEM((4, 4, 32, 1536), BF16),
+            pltpu.VMEM((4, 32, 1536), BF16),
+            pltpu.VMEM((4, 4, 32, 1536), BF16),
+            pltpu.VMEM((2, 2, 32, 1536), BF16),
+            pltpu.VMEM((2, 4, 32, 1536), BF16),
+            pltpu.VMEM((2, 16, 1536), BF16),
+            pltpu.VMEM((2, 32, 1536), BF16),
             pltpu.VMEM((8, 48, 1536), BF16),
             pltpu.VMEM((8, 8, 48, 384), BF16),
             pltpu.VMEM((8, 48, 3072), BF16),
             pltpu.VMEM((2, 384, 768), BF16),
-            pltpu.VMEM((8, 48, 3072), F32),
             pltpu.VMEM((12, 48, 128), F32),
             pltpu.VMEM((12, 48, 128), F32),
             pltpu.VMEM((12, 48, 128), F32),
@@ -599,7 +706,7 @@
             pltpu.VMEM((8, 24, 128), F32),
             pltpu.VMEM((8, 24, 128), F32),
             pltpu.VMEM((8, 24, 128), F32),
-            pltpu.SemaphoreType.DMA((13,)),
+            pltpu.SemaphoreType.DMA((12,)),
             pltpu.SemaphoreType.DMA((N_COPY,)),
             pltpu.SemaphoreType.DMA((N_COPY,)),
         ],

time: 105 us -> 97.9 us (0.932)
  Pallas kernels: 102 us -> 95.1 us
    pallas_call x1, Pallas kernels: 102 us -> 95.1 us  [per_device(): pl.pallas_call(kernel, out_shape=jax.ShapeDtypeStruct((2, 24, 64), F32),...]
where the time goes in v3:
time: 97.9 us; the launch traced here: 97.7 us
  Pallas kernels  95.1 us (97%)
  local copies, waits for them, and re-layouts  1.33 us (1%)
  between operations  1.29 us (1%)
    pallas_call x1, Pallas kernels, per_device(): pl.pallas_call(kernel, out_shape=jax.ShapeDtypeStruct((2, 24, 64), F32),...  95.1 us

profile of v3, /device:TPU:1, one launch (start us, length us, event | category | flops | bytes accessed | tf_op | source)
XLA Modules:
  0.0 97.7 jit_solution(1251453794027170410)
XLA Ops:
  1.3 95.1 %shard_map.158 = f32[2,24,64]{2,1,0:T(8,128)} custom-call(s32[8]{0:T(128)} %len_ref.1, s32[1]{0:T(128)S(6)} %copy.17.step_ref, s32[1,96]{1,0:T(1,128)} %slot_ref.1, s32[3,1,6]{2,1,0:T(1,128)} %pos_ref.1, bf16[48,1536]{1,0:T(8,128)(2,1)} %bitcast.20, bf16[2,512,1536]{2,1,0:T(8,128)(2,1)} %bitcast.15, bf16[2,768,1536]{2,1,0:T(8,128)(2,1)} %bitcast.14, ...), custom_call_target="tpu_custom_call" | custom-call | tf_op jit(solution)/shard_map/pallas_call | solution.py:673
  96.4 1.3 %fusion = (f32[1,24,64]{2,1,0:T(8,128)}, f32[1,24,64]{2,1,0:T(8,128)}) fusion(f32[2,24,64]{2,1,0:T(8,128)} %shard_map.158), kind=kLoop, calls=%fused_computation | loop fusion | bytes 24576 | tf_op jit(solution)/shard_map/slice | solution.py:733

commit v4 on v3

--- a/solution.py
+++ b/solution.py
@@ -19,15 +19,15 @@
 NEG = -jnp.inf
 SKIP = frozenset()
 
-ITEMS = ("fresh", "out", "up0", "up1")
-OPS = ("1R", "1L", "1RR", "1LL", "2R", "2L", "2RR", "2LL", "Xa", "Xb", "Xc", "Ya", "Yb", "Yc")
+ITEMS = ("out", "up0", "up1")
+OPS = ("1R", "1L", "1O", "2O", "1RR", "1LL", "2R", "2L", "2RR", "2LL", "Xa", "Xb", "Xc", "Ya", "Yb", "Yc")
 N_PLANE = len(ITEMS) * len(OPS)
 RING_OPS = ("R1", "R2", "R3", "R4", "L1", "L2", "L3", "L4")
 N_RING = 4 * len(RING_OPS)
 N_VEL = 8
-FOLD_OPS = ("1R", "1L", "2R", "2L", "3R", "3L", "4R", "4L", "5R", "5L", "5RR", "5LL", "6R", "6L", "6RR", "6LL")
+FOLD_OPS = ("1R", "1L", "2R", "2L", "3R", "3L", "3O", "4R", "4L", "4O", "5R", "5L", "5RR", "5LL")
 N_FOLD = len(FOLD_OPS)
-N_COPY = N_PLANE + N_RING + N_VEL + N_FOLD + 1
+N_COPY = N_PLANE + N_RING + N_VEL + N_FOLD + 32 + 1
 
 
 def nt_dot(a, b):
@@ -77,7 +77,6 @@
     gin1,
     gin2,
     gin3,
-    gin4,
     abuf,
     rbuf,
     nbuf,
@@ -111,6 +110,9 @@
         loads[name] = pltpu.make_async_copy(src, dst, load_sem.at[len(loads)])
         loads[name].start()
 
+    load("mod", mod_hbm.at[c], mod)
+    load("wf", wf_hbm, wf)
+    load("down", down_hbm, down)
     load("q", q_hbm, q_ref)
     load("tk", text_hbm.at[0], text.at[0])
     load("ik", img_hbm.at[0], img.at[0])
@@ -119,54 +121,44 @@
     load("out", out_hbm, obuf.at[y, x])
     for half in (0, 1):
         load("up%d" % half, up_hbm.at[:, :, pl.ds(768 * half, 768)], ubuf.at[half, y, x])
-    load("down", down_hbm, down)
     load("stream", stream_hbm, stream)
-    load("mod", mod_hbm.at[c], mod)
-    load("wf", wf_hbm, wf)
 
     def plane(item, op, core):
         half = int(item[-1]) if item[-1] in "01" else 0
-        if item == "fresh":
-            buf, shard = fbuf, None
-        elif item == "out":
+        if item == "out":
             buf, shard = obuf, out_hbm.at[core]
         else:
             buf, shard = ubuf.at[half], up_hbm.at[core, :, pl.ds(768 * half, 768)]
         u, v = (x, y) if core == 0 else (y, x)
-        own = () if item == "fresh" else (core,)
-
         def mod4(i):
             return lax.rem(i + 4, 4)
 
         def at(uu, vv, extra=()):
             where = (vv, uu) if core == 0 else (uu, vv)
-            return buf.at[where + own + extra]
+            return buf.at[where + (core,) + extra]
 
         def device(uu, vv):
             return {"seq": vv * 4 + uu if core == 0 else uu * 4 + vv}
 
-        if item == "fresh":
-            halves = ((slice(None), pl.ds(0, 768)), (slice(None), pl.ds(768, 768)))
-        elif item == "out":
+        if item == "out":
             halves = ((pl.ds(0, 32),), (pl.ds(32, 16),))
         else:
             halves = ((pl.ds(0, 48),), (pl.ds(48, 48),))
         right1, left1 = device(mod4(u + 1), v), device(mod4(u - 1), v)
         right2, left2 = device(u, mod4(v + 1)), device(u, mod4(v - 1))
         every = slice(None)
-        if op in ("1R", "1L"):
-            dst = at(u, v)
-            src = dst if item == "fresh" else shard
-            dev = right1 if op == "1R" else left1
+        if op in ("1R", "1L", "1O"):
+            src, dst = shard, at(u, v)
+            dev = {"R": right1, "L": left1, "O": device(mod4(u + 2), v)}[op[1]]
         elif op == "1RR":
             src = dst = at(mod4(u - 1), v, halves[0])
             dev = right1
         elif op == "1LL":
             src = dst = at(mod4(u + 1), v, halves[1])
             dev = left1
-        elif op in ("2R", "2L"):
+        elif op in ("2R", "2L", "2O"):
             src = dst = at(every, v)
-            dev = right2 if op == "2R" else left2
+            dev = {"R": right2, "L": left2, "O": device(u, mod4(v + 2))}[op[1]]
         elif op == "2RR":
             src = dst = at(pl.ds(0, 2), mod4(v - 1))
             dev = right2
@@ -208,26 +200,31 @@
         if steps:
             both(act)
 
+    def out_first():
+        serve(("out", None, "1R 1L 1O"))
+
+    def out_second():
+        loads["out"].wait()
+        serve(("out", "1R", "Xa"), ("out", "1L", "Xb"), ("out", "1O", "2R 2L 2O Xc"))
+
+    def out_third():
+        serve(("out", "2R", "Ya"), ("out", "2L", "Yb"), ("out", "2O", "Yc"))
+
     def first(item):
         serve((item, None, "1R 1L"))
 
     def second(item):
-        hand = item != "fresh"
-        serve((item, "1R", "1RR Xa" if hand else "1RR"), (item, "1L", "1LL Xb" if hand else "1LL"))
+        serve((item, "1R", "1RR Xa"), (item, "1L", "1LL Xb"))
 
     def third(item):
-        if item in loads:
-            loads[item].wait()
-        hand = item != "fresh"
-        serve((item, "1RR", ""), (item, "1LL", "2R 2L Xc" if hand else "2R 2L"))
+        loads[item].wait()
+        serve((item, "1RR", ""), (item, "1LL", "2R 2L Xc"))
 
     def fourth(item):
-        hand = item != "fresh"
-        serve((item, "2R", "2RR Ya" if hand else "2RR"), (item, "2L", "2LL Yb" if hand else "2LL"))
+        serve((item, "2R", "2RR Ya"), (item, "2L", "2LL Yb"))
 
     def fifth(item):
-        hand = item != "fresh"
-        serve((item, "2RR", ""), (item, "2LL", "Yc" if hand else ""))
+        serve((item, "2RR", ""), (item, "2LL", "Yc"))
 
     def take(item):
         if item in SKIP:
@@ -245,23 +242,18 @@
         def mod4(i):
             return lax.rem(i + 4, 4)
 
-        right = "R" in op
-        one = 1 if right else -1
-        along_u = op[0] in "126"
-        uu, vv = (mod4(u + one), v) if along_u else (u, mod4(v + one))
+        one = {"R": 1, "L": -1, "O": 2}[op[1]]
+        side = "RLO".index(op[1])
+        uu, vv = (mod4(u + one), v) if op[0] in "125" else (u, mod4(v + one))
         dev = {"seq": vv * 4 + uu if core == 0 else uu * 4 + vv}
-        side = 0 if right else 1
         if op[0] == "1":
             src, dst = gpart.at[mod4(u + 2), pl.ds(2 * side, 2)], gin1.at[side]
         elif op[0] == "2":
             src, dst = gpart.at[mod4(u + one)], gin2.at[side]
         elif op[0] == "3":
-            src, dst = gmid.at[mod4(v + 2), pl.ds(16 * side, 16)], gin3.at[side]
+            src, dst = gmid.at[mod4(v + one)], gin3.at[side]
         elif op[0] == "4":
-            src, dst = gmid.at[mod4(v + one)], gin4.at[side]
-        elif op[0] == "5":
-            src = gfull.at[u, v] if len(op) == 2 else gfull.at[u, mod4(v - one), pl.ds(16 * side, 16)]
-            dst = src
+            src = dst = gfull.at[u, v]
         else:
             src = gfull.at[u] if len(op) == 2 else gfull.at[mod4(u - one), pl.ds(2 * side, 2)]
             dst = src
@@ -314,17 +306,11 @@
             total = gpart[u, i].astype(F32) + gin2[0, i].astype(F32) + gin2[1, i].astype(F32)
             gmid[i] = total.astype(BF16)
 
-    def add3(side):
-        def add(core):
-            v = across(core, 1 - 2 * side)[1]
-            rows = pl.ds(16 * side, 16)
-            gmid[v, rows] = (gmid[v, rows].astype(F32) + gin3[side].astype(F32)).astype(BF16)
-
-        return add
-
-    def add4(core):
+    def add3(core):
         u, v = across(core, 0)
-        total = gmid[v].astype(F32) + gin4[0].astype(F32) + gin4[1].astype(F32)
+        total = gmid[v].astype(F32)
+        for side in range(3):
+            total = total + gin3[side].astype(F32)
         gfull[u, v] = total.astype(BF16)
 
     def fold_local():
@@ -377,11 +363,33 @@
             if k < 3 or (k == 3 and chunk == "RL".index(side)):
                 ring_go(which, chunk, side + str(k + 1))
 
+    def fresh_copy(half, step):
+        spot = fbuf.at[y, x, :, pl.ds(768 * half, 768)]
+        index = N_COPY - 33 + 16 * half + step
+        return pltpu.make_async_remote_copy(
+            src_ref=spot,
+            dst_ref=spot,
+            send_sem=send_sem.at[index],
+            recv_sem=recv_sem.at[index],
+            device_id={"seq": lax.rem(y + step // 4, 4) * 4 + lax.rem(x + step % 4, 4)},
+            device_id_type=MESH,
+        )
+
+    def fresh_go(half):
+        if "fresh" not in SKIP:
+            for step in (10, 9, 11, 6, 14, 5, 7, 13, 15, 2, 8, 1, 3, 4, 12):
+                fresh_copy(half, step).start()
+                started.append(fresh_copy(half, step))
+
+    def fresh_wait(half):
+        if "fresh" not in SKIP:
+            for step in range(1, 16):
+                fresh_copy(half, step).wait_recv()
+
     barrier = pltpu.get_barrier_semaphore()
     greeted = [{"cfg": 1 - c}]
-    for step in (1, 3):
-        greeted.append({"seq": y * 4 + lax.rem(x + step, 4)})
-        greeted.append({"seq": lax.rem(y + step, 4) * 4 + x})
+    for step in range(1, 16):
+        greeted.append({"seq": lax.rem(s + step, 16)})
     for step in range(1, 8):
         greeted.append({"req": ring8(step)})
     for device in greeted:
@@ -417,8 +425,9 @@
 
     pl.semaphore_wait(barrier, len(greeted))
 
-    first("fresh")
-    first("out")
+    out_first()
+    fresh_go(0)
+    fresh_go(1)
 
     length = len_ref[z]
     key_place = lax.broadcasted_iota(jnp.int32, (8, 768), 1)
@@ -514,79 +523,72 @@
         vel[r, :, 0:64] += rows
         return carry
 
+    for name in ("mod", "wf", "down"):
+        loads[name].wait()
+    fold_local()
     for name in ("q", "tk", "ik", "tv", "iv"):
         loads[name].wait()
-    cached_heads(0, 1, 2)
-    second("fresh")
+    cached_heads(0, 1, 2, 3)
     first("up0")
-    cached_heads(3, 4, 5)
-    third("fresh")
-    second("out")
     first("up1")
-    cached_heads(6, 7, 8)
-    third("out")
-    second("up0")
-    cached_heads(9, 10, 11)
-    fourth("fresh")
-    third("up0")
-    second("up1")
-    fifth("fresh")
+    cached_heads(4, 5, 6, 7)
+    out_second()
+    cached_heads(8, 9, 10, 11)
+    fresh_wait(0)
     fresh_heads(0, 1, 2, 3, 4, 5)
     ring_go(0, 0, "R1", "L1")
+    second("up0")
+    second("up1")
+    fresh_wait(1)
     fresh_heads(6, 7, 8, 9, 10, 11)
     ring_go(0, 1, "R1", "L1")
-    fourth("out")
-    third("up1")
-    for name in ("stream", "mod", "wf", "down"):
-        loads[name].wait()
+    fold_step((None, None, "1R 1L"))
+    out_third()
+    third("up0")
     hop(0, 0, 1)
     hop(0, 1, 1)
-    fifth("out")
-    fold_local()
-    fold_step((None, None, "1R 1L"))
+    third("up1")
+    fold_step(("1R", add1(0), "2R"), ("1L", add1(1), "2L"))
+    loads["stream"].wait()
     take("out")
     project(0)
     hop(0, 0, 2)
     hop(0, 1, 2)
-    project(-1, 1)
-    fourth("up0")
+    project(-1, 1, 2)
+    ring_go(1, 0, "R1", "L1")
     hop(0, 0, 3)
     hop(0, 1, 3)
-    project(2)
-    ring_go(1, 0, "R1", "L1")
-    project(-2)
-    fold_step(("1R", add1(0), "2R"), ("1L", add1(1), "2L"))
+    project(-2, 3, -3)
     hop(0, 0, 4)
     hop(0, 1, 4)
-    project(3, 4, -3)
+    project(4)
     ring_go(1, 1, "R1", "L1")
+    fold_step(("2R", None, ""), ("2L", add2, "3R 3L 3O"))
+    fourth("up0")
+    hop(1, 0, 1)
+    fold_step(("3R", None, ""), ("3L", None, ""), ("3O", add3, "4R 4L 4O"))
+    hop(1, 1, 1)
+    hop(1, 0, 2)
+    fold_step(("4R", None, ""), ("4L", None, ""), ("4O", None, "5R 5L"))
+    hop(1, 1, 2)
+    fourth("up1")
     fifth("up0")
-    fourth("up1")
-    hop(1, 0, 1)
-    hop(1, 1, 1)
-    fold_step(("2R", None, ""), ("2L", add2, "3R 3L"))
-    hop(1, 0, 2)
-    fold_step(("3R", add3(0), "4R"), ("3L", add3(1), "4L"))
-    hop(1, 1, 2)
-    fold_step(("4R", None, ""), ("4L", add4, "5R 5L"))
+    hop(1, 0, 3)
+    hop(1, 1, 3)
+    fold_step(("5R", None, "5RR"), ("5L", None, "5LL"))
     fifth("up1")
     vel[...] = jnp.zeros_like(vel)
-    hop(1, 0, 3)
-    fold_step(("5R", None, "5RR"), ("5L", None, "5LL"))
-    hop(1, 1, 3)
-    fold_step(("5RR", None, ""), ("5LL", None, "6R 6L"))
     hop(1, 0, 4)
     hop(1, 1, 4)
     if "norm" not in SKIP:
         lax.fori_loop(0, 8, normalize, 0)
-    fold_step(("6R", None, "6RR"), ("6L", None, "6LL"))
     own = jnp.concatenate([rbuf[b, lax.rem(z - b + 9, 8)] for b in range(8)], axis=-1)
     vel[z, :, 0:64] = nt_dot(own, wf[...])
     take("up0")
     up_half(0)
     take("up1")
     up_half(1)
-    fold_step(("6RR", None, ""), ("6LL", None, ""))
+    fold_step(("5RR", None, ""), ("5LL", None, ""))
     if "mm" not in SKIP:
         lax.fori_loop(0, 8, velocity, 0)
 
@@ -692,8 +694,7 @@
             pltpu.VMEM((4, 4, 32, 1536), BF16),
             pltpu.VMEM((2, 2, 32, 1536), BF16),
             pltpu.VMEM((2, 4, 32, 1536), BF16),
-            pltpu.VMEM((2, 16, 1536), BF16),
-            pltpu.VMEM((2, 32, 1536), BF16),
+            pltpu.VMEM((3, 32, 1536), BF16),
             pltpu.VMEM((8, 48, 1536), BF16),
             pltpu.VMEM((8, 8, 48, 384), BF16),
             pltpu.VMEM((8, 48, 3072), BF16),

time: 97.9 us -> 93.5 us (0.955)
  Pallas kernels: 95.1 us -> 90.7 us
    pallas_call x1, Pallas kernels: 95.1 us -> 90.7 us  [per_device(): pl.pallas_call(kernel, out_shape=jax.ShapeDtypeStruct((2, 24, 64), F32),...]
where the time goes in v4:
time: 93.5 us; the launch traced here: 93.3 us
  Pallas kernels  90.7 us (97%)
  local copies, waits for them, and re-layouts  1.33 us (1%)
  between operations  1.29 us (1%)
    pallas_call x1, Pallas kernels, per_device(): pl.pallas_call(kernel, out_shape=jax.ShapeDtypeStruct((2, 24, 64), F32),...  90.7 us

profile of v4, /device:TPU:1, one launch (start us, length us, event | category | flops | bytes accessed | tf_op | source)
XLA Modules:
  0.0 93.3 jit_solution(8150831909828285623)
XLA Ops:
  1.3 90.7 %shard_map.158 = f32[2,24,64]{2,1,0:T(8,128)} custom-call(s32[8]{0:T(128)} %len_ref.1, s32[1]{0:T(128)S(6)} %copy.17.step_ref, s32[1,96]{1,0:T(1,128)} %slot_ref.1, s32[3,1,6]{2,1,0:T(1,128)} %pos_ref.1, bf16[48,1536]{1,0:T(8,128)(2,1)} %bitcast.20, bf16[2,512,1536]{2,1,0:T(8,128)(2,1)} %bitcast.15, bf16[2,768,1536]{2,1,0:T(8,128)(2,1)} %bitcast.14, ...), custom_call_target="tpu_custom_call" | custom-call | tf_op jit(solution)/shard_map/pallas_call | solution.py:675
  92.0 1.3 %fusion = (f32[1,24,64]{2,1,0:T(8,128)}, f32[1,24,64]{2,1,0:T(8,128)}) fusion(f32[2,24,64]{2,1,0:T(8,128)} %shard_map.158), kind=kLoop, calls=%fused_computation | loop fusion | bytes 24576 | tf_op jit(solution)/shard_map/slice | solution.py:734

commit v5 on v4

--- a/solution.py
+++ b/solution.py
@@ -537,12 +537,12 @@
     fresh_wait(0)
     fresh_heads(0, 1, 2, 3, 4, 5)
     ring_go(0, 0, "R1", "L1")
-    second("up0")
-    second("up1")
     fresh_wait(1)
     fresh_heads(6, 7, 8, 9, 10, 11)
     ring_go(0, 1, "R1", "L1")
     fold_step((None, None, "1R 1L"))
+    second("up0")
+    second("up1")
     out_third()
     third("up0")
     hop(0, 0, 1)
@@ -564,8 +564,8 @@
     project(4)
     ring_go(1, 1, "R1", "L1")
     fold_step(("2R", None, ""), ("2L", add2, "3R 3L 3O"))
+    hop(1, 0, 1)
     fourth("up0")
-    hop(1, 0, 1)
     fold_step(("3R", None, ""), ("3L", None, ""), ("3O", add3, "4R 4L 4O"))
     hop(1, 1, 1)
     hop(1, 0, 2)

time: 93.5 us -> 92 us (0.984)
  Pallas kernels: 90.7 us -> 89.1 us
    pallas_call x1, Pallas kernels: 90.7 us -> 89.1 us  [per_device(): pl.pallas_call(kernel, out_shape=jax.ShapeDtypeStruct((2, 24, 64), F32),...]
where the time goes in v5:
time: 92 us; the launch traced here: 91.7 us
  Pallas kernels  89.1 us (97%)
  local copies, waits for them, and re-layouts  1.33 us (1%)
  between operations  1.29 us (1%)
    pallas_call x1, Pallas kernels, per_device(): pl.pallas_call(kernel, out_shape=jax.ShapeDtypeStruct((2, 24, 64), F32),...  89.1 us

profile of v5, /device:TPU:1, one launch (start us, length us, event | category | flops | bytes accessed | tf_op | source)
XLA Modules:
  0.0 91.7 jit_solution(12602713071182797381)
XLA Ops:
  1.3 89.1 %shard_map.158 = f32[2,24,64]{2,1,0:T(8,128)} custom-call(s32[8]{0:T(128)} %len_ref.1, s32[1]{0:T(128)S(6)} %copy.17.step_ref, s32[1,96]{1,0:T(1,128)} %slot_ref.1, s32[3,1,6]{2,1,0:T(1,128)} %pos_ref.1, bf16[48,1536]{1,0:T(8,128)(2,1)} %bitcast.20, bf16[2,512,1536]{2,1,0:T(8,128)(2,1)} %bitcast.15, bf16[2,768,1536]{2,1,0:T(8,128)(2,1)} %bitcast.14, ...), custom_call_target="tpu_custom_call" | custom-call | tf_op jit(solution)/shard_map/pallas_call | solution.py:675
  90.4 1.3 %fusion = (f32[1,24,64]{2,1,0:T(8,128)}, f32[1,24,64]{2,1,0:T(8,128)}) fusion(f32[2,24,64]{2,1,0:T(8,128)} %shard_map.158), kind=kLoop, calls=%fused_computation | loop fusion | bytes 24576 | tf_op jit(solution)/shard_map/slice | solution.py:734
